TPU v7x, 128 devices: a whole 4x4x4 slice. The times are simulated.
128 devices in a mesh: samp: 32 (over y, x, core), slab: 4 (over z).
Axes of the slice: x: 4, y: 4, z: 4, core: 2. Of those that a mesh axis runs over, the one named last changes fastest.
Arguments:
- ld_blocks: bfloat16 [4, 64, 768, 768], P('slab', 'samp'), may hold values from -1 to 1, as said below
- marginal: float32 [4, 49152], P('slab', 'samp'), may hold values from -1.8 to 1.8
- normals: float32 [2, 4, 49152], P(None, 'slab', 'samp'), may hold values from -6 to 6
- block_len: int32 [64], P('samp'), may hold values from 1 to 768, 36864 in all
- scale_start: float32 [49152], P('samp'), may hold values from 0.2 to 5
- ancestry_weight: float32 [4], replicated, may hold values from 4 to 64
- dosage: bfloat16 [4096, 49152], P('samp', 'slab'), may hold values from 0 to 2
Outputs:
- effects: float32 [4, 49152], P('slab', 'samp')
- shrink: float32 [49152], P('samp')
- scores: float32 [4096, 4], P('samp', 'slab')
Inputs may be any that keep to these rules, and one draw needn't show every extreme that they name: `block_len`: the block lengths sum to 36864; the longest is exactly 768. `ld_blocks`: every block is symmetric with unit diagonal, and it and each of its leading principal submatrices is positive definite.
All inputs are finite; a program needn't handle non-finite values.
Results may differ from a plain program's by a relative error of at most 0.0031.
Values may be sent and summed in bfloat16 or wider, within the bound.
A program may use at most 128 MiB of HBM per device.

v0:
```python
import jax
import jax.numpy as jnp
from jax import lax
from jax.sharding import PartitionSpec as P

SWEEPS = 2


shape_total = 1.5
global_shrink = 0.01


def mean_rounded(stacked):
    total = stacked[:, 0]
    total = total + stacked[:, 1]
    return (total / stacked.shape[1]).astype(jnp.bfloat16)


def score_terms(columns, weights):
    product = lax.dot_general(
        columns, weights, (((1,), (1,)), ((), ())), preferred_element_type=jnp.float32
    )
    return (product, jnp.sum(weights.astype(jnp.float32), axis=1))


def per_device(ld_blocks, marginal, normals, block_len, scale_start, ancestry_weight, dosage):
    slot_count = ld_blocks.shape[1]
    block_size = ld_blocks.shape[2]
    ancestries = ancestry_weight.shape[0]
    own_index = lax.axis_index("slab")
    weight = lax.dynamic_index_in_dim(ancestry_weight, own_index, 0, keepdims=False)
    position = jnp.arange(block_size, dtype=jnp.int32)
    live_rows = (position[None, :] < block_len[:, None]).astype(jnp.float32)
    correlation = ld_blocks[0].astype(jnp.float32) * (live_rows[:, :, None] * live_rows[:, None, :])
    identity = jnp.eye(block_size, dtype=jnp.float32)
    targets = marginal[0].reshape(slot_count, block_size) * live_rows
    shrink = scale_start.reshape(slot_count, block_size)
    shrink_rate = shape_total / (shrink + global_shrink)
    variance = jnp.ones((), jnp.float32)
    local_live = jnp.sum(live_rows)
    live_total = local_live
    drawn = []
    for sweep_index in range(SWEEPS):
        inverse = 1.0 / shrink
        system = (
            correlation
            + identity[None, :, :] * (live_rows * inverse + (1.0 - live_rows))[:, None, :]
        )
        factor = jnp.linalg.cholesky(system)
        forward = lax.linalg.triangular_solve(
            factor, targets[:, :, None], left_side=True, lower=True
        )[:, :, 0]
        noise_level = jnp.sqrt(variance / weight)
        forward = (
            forward
            + noise_level * normals[sweep_index, 0].reshape(slot_count, block_size) * live_rows
        )
        effect = lax.linalg.triangular_solve(
            factor, forward[:, :, None], left_side=True, lower=True, transpose_a=True
        )[:, :, 0]
        fitted = jnp.einsum("sij,sj->si", correlation, effect, precision=lax.Precision.HIGHEST)
        misfit = targets - fitted
        stat_row = jnp.stack(
            [jnp.sum(misfit * misfit), jnp.sum(effect * effect * inverse * live_rows), local_live]
        )
        totals = lax.psum(stat_row, "samp")
        variance = (totals[0] + totals[1] + 1.0) / (totals[2] + 1.0)
        pooled = lax.psum(weight * effect * effect / variance, "slab")
        live_total = totals[2]
        shrink = (pooled + 1.0) / (2.0 + jnp.sqrt(4.0 + 2.0 * shrink_rate * (pooled + 1.0)))
        shrink_rate = shape_total / (shrink + global_shrink)
        drawn.append(effect.reshape(1, slot_count * block_size))
    total = drawn[0]
    sweep_index = 1
    total = total + drawn[sweep_index]
    effects = total / SWEEPS
    stacked = jnp.concatenate(drawn, axis=0)
    slab_count = lax.axis_size("slab")
    samp_count = lax.axis_size("samp")
    quarter = slot_count * block_size // slab_count
    spread = lax.all_gather(stacked, "samp", axis=1, tiled=True)
    layout = spread.reshape(1, SWEEPS, samp_count, slab_count, quarter)
    received = lax.all_to_all(layout, "slab", split_axis=3, concat_axis=0, tiled=True)
    weights = mean_rounded(received.reshape(ancestries, SWEEPS, samp_count * quarter))
    products, column_sums = score_terms(dosage, weights)
    partial_value = products - column_sums[None, :]
    scores = lax.psum_scatter(partial_value, "slab", scatter_dimension=1, tiled=True) / jnp.sqrt(
        live_total
    )
    return (effects, shrink.reshape(slot_count * block_size), scores)


def solution(mesh):
    return jax.shard_map(
        per_device,
        mesh=mesh,
        in_specs=(
            P("slab", "samp", None, None),
            P("slab", "samp"),
            P(None, "slab", "samp"),
            P("samp"),
            P("samp"),
            P(),
            P("samp", "slab"),
        ),
        out_specs=(P("slab", "samp"), P("samp"), P("samp", "slab")),
        check_vma=False,
    )
```

profile of v0, /device:TPU:1, one launch (start us, length us, event | category | flops | bytes accessed | tf_op | source)
XLA Modules:
  0.0 1178.4 jit_solution(14147899627568268930)
XLA Ops:
  6.4 4.3 copy.120
  11.4 4.2 multiply_add_fusion.1
  15.7 6.2 copy.121
  21.8 4.4 fusion.1
  28.3 23.5 %custom-call.57 = f32[2,128,128]{2,1,0:T(8,128)S(1)} custom-call(f32[2,128,128]{2,1,0:T(8,128)S(1)} %cholesky.662), custom_call_target="Cholesky" | custom-call | tf_op jit(solution)/shard_map/jit(cholesky)/cholesky | solution.py:49
  51.8 19.7 %custom-call.58 = f32[2,1,128,128]{2,3,1,0:T(8,128)S(1)} custom-call(f32[2,1,128,128]{3,2,1,0:T(8,128)S(1)} %select_bitcast_fusion.9), custom_call_target="InvertDiagBlocksLowerTriangular" | custom-call | tf_op jit(solution)/shard_map/jit(cholesky)/cholesky | solution.py:49
  79.4 23.7 %custom-call.59 = f32[2,128,128]{2,1,0:T(8,128)S(1)} custom-call(f32[2,128,128]{2,1,0:T(8,128)S(1)} %cholesky.666), custom_call_target="Cholesky" | custom-call | tf_op jit(solution)/shard_map/jit(cholesky)/cholesky | solution.py:49
  103.9 19.7 %custom-call.60 = f32[2,1,128,128]{2,3,1,0:T(8,128)S(1)} custom-call(f32[2,1,128,128]{3,2,1,0:T(8,128)S(1)} %get-tuple-element.95), custom_call_target="InvertDiagBlocksLowerTriangular" | custom-call | tf_op jit(solution)/shard_map/jit(cholesky)/cholesky | solution.py:49
  129.4 23.5 %custom-call.61 = f32[2,128,128]{2,1,0:T(8,128)S(1)} custom-call(f32[2,128,128]{2,1,0:T(8,128)S(1)} %cholesky.671), custom_call_target="Cholesky" | custom-call | tf_op jit(solution)/shard_map/jit(cholesky)/cholesky | solution.py:49
  153.6 20.9 %custom-call.62 = f32[2,1,128,128]{2,3,1,0:T(8,128)S(1)} custom-call(f32[2,1,128,128]{3,2,1,0:T(8,128)} %get-tuple-element.93), custom_call_target="InvertDiagBlocksLowerTriangular" | custom-call | tf_op jit(solution)/shard_map/jit(cholesky)/cholesky | solution.py:49
  180.2 24.9 %custom-call.63 = f32[2,128,128]{2,1,0:T(8,128)} custom-call(f32[2,128,128]{2,1,0:T(8,128)} %cholesky.676), custom_call_target="Cholesky" | custom-call | tf_op jit(solution)/shard_map/jit(cholesky)/cholesky | solution.py:49
  206.7 21.1 %custom-call.64 = f32[2,1,128,128]{2,3,1,0:T(8,128)} custom-call(f32[2,1,128,128]{3,2,1,0:T(8,128)} %get-tuple-element.91), custom_call_target="InvertDiagBlocksLowerTriangular" | custom-call | tf_op jit(solution)/shard_map/jit(cholesky)/cholesky | solution.py:49
  233.0 24.4 %custom-call.65 = f32[2,128,128]{2,1,0:T(8,128)S(1)} custom-call(f32[2,128,128]{2,1,0:T(8,128)} %cholesky.681), custom_call_target="Cholesky" | custom-call | tf_op jit(solution)/shard_map/jit(cholesky)/cholesky | solution.py:49
  258.2 21.1 %custom-call.66 = f32[2,1,128,128]{2,3,1,0:T(8,128)} custom-call(f32[2,1,128,128]{3,2,1,0:T(8,128)} %get-tuple-element.89), custom_call_target="InvertDiagBlocksLowerTriangular" | custom-call | tf_op jit(solution)/shard_map/jit(cholesky)/cholesky | solution.py:49
  283.3 23.5 %custom-call.67 = f32[2,128,128]{2,1,0:T(8,128)S(1)} custom-call(f32[2,128,128]{2,1,0:T(8,128)S(1)} %convolution_subtract_fusion.9), custom_call_target="Cholesky" | custom-call | tf_op jit(solution)/shard_map/jit(cholesky)/cholesky | solution.py:49
  309.1 5.3 select_select_fusion.1
  315.4 22.0 %while.8 = (s32[]{:T(128)}, f32[2,768,768]{2,1,0:T(8,128)}, s32[6,2]{0,1:T(2,128)S(1)}, f32[6,2,128,128]{3,2,0,1:T(8,128)}, s32[]{:T(128)}) while((s32[]{:T(128)}, f32[2,768,768]{2,1,0:T(8,128)}, s32[6,2]{0,1:T(2,128)S(1)}, f32[6,2,128,128]{3,2,0,1:T(8,128)}, s32[]{:T(128)}) %tuple.92), condition=%wide.while_cond.1, body=%wide.while_body.1.sunk | while | flops 2 | bytes 263777 | solution.py:58
  316.1 3.0 bitcast_dynamic-update-slice_fusion.4
  319.8 3.0 bitcast_dynamic-update-slice_fusion.4
  323.5 3.0 bitcast_dynamic-update-slice_fusion.4
  327.1 3.0 bitcast_dynamic-update-slice_fusion.4
  330.8 3.0 bitcast_dynamic-update-slice_fusion.4
  337.5 119.5 %custom-call.69 = f32[2,6,128,128]{2,3,1,0:T(8,128)} custom-call(f32[2,6,128,128]{3,2,1,0:T(8,128)} %bitcast.493), custom_call_target="InvertDiagBlocksLowerTriangular" | custom-call | tf_op jit(solution)/shard_map/triangular_solve/custom-call.12 | solution.py:58
  487.5 4.6 fusion.3
  494.9 63.8 %psum.28 = f32[3]{0:T(128)S(1)} all-reduce(f32[3]{0:T(128)S(1)} %maximum_maximum_fusion), channel_id=1, replica_groups=mesh['samp'=32,'slab'=4] {'samp'}, use_global_device_ids=true, to_apply=%region_15.19 | all-reduce | flops 3 | bytes 24 | tf_op jit(solution)/shard_map/psum | solution.py:66
  563.3 9.8 psum.29
  573.8 4.7 multiply_add_fusion
  578.5 6.1 copy.134
  584.6 4.4 fusion
  591.1 23.5 %custom-call.70 = f32[2,128,128]{2,1,0:T(8,128)S(1)} custom-call(f32[2,128,128]{2,1,0:T(8,128)S(1)} %cholesky.685), custom_call_target="Cholesky" | custom-call | tf_op jit(solution)/shard_map/jit(cholesky)/cholesky | solution.py:49
  617.1 19.7 %custom-call.71 = f32[2,1,128,128]{2,3,1,0:T(8,128)S(1)} custom-call(f32[2,1,128,128]{3,2,1,0:T(8,128)S(1)} %select_bitcast_fusion.4), custom_call_target="InvertDiagBlocksLowerTriangular" | custom-call | tf_op jit(solution)/shard_map/jit(cholesky)/cholesky | solution.py:49
  642.2 23.6 %custom-call.72 = f32[2,128,128]{2,1,0:T(8,128)S(1)} custom-call(f32[2,128,128]{2,1,0:T(8,128)S(1)} %cholesky.689), custom_call_target="Cholesky" | custom-call | tf_op jit(solution)/shard_map/jit(cholesky)/cholesky | solution.py:49
  666.6 19.7 %custom-call.73 = f32[2,1,128,128]{2,3,1,0:T(8,128)S(1)} custom-call(f32[2,1,128,128]{3,2,1,0:T(8,128)S(1)} %get-tuple-element.86), custom_call_target="InvertDiagBlocksLowerTriangular" | custom-call | tf_op jit(solution)/shard_map/jit(cholesky)/cholesky | solution.py:49
  692.1 23.5 %custom-call.74 = f32[2,128,128]{2,1,0:T(8,128)S(1)} custom-call(f32[2,128,128]{2,1,0:T(8,128)S(1)} %cholesky.694), custom_call_target="Cholesky" | custom-call | tf_op jit(solution)/shard_map/jit(cholesky)/cholesky | solution.py:49
  716.3 20.7 %custom-call.75 = f32[2,1,128,128]{2,3,1,0:T(8,128)S(1)} custom-call(f32[2,1,128,128]{3,2,1,0:T(8,128)} %get-tuple-element.84), custom_call_target="InvertDiagBlocksLowerTriangular" | custom-call | tf_op jit(solution)/shard_map/jit(cholesky)/cholesky | solution.py:49
  742.7 24.9 %custom-call.76 = f32[2,128,128]{2,1,0:T(8,128)} custom-call(f32[2,128,128]{2,1,0:T(8,128)} %cholesky.699), custom_call_target="Cholesky" | custom-call | tf_op jit(solution)/shard_map/jit(cholesky)/cholesky | solution.py:49
  769.2 21.1 %custom-call.77 = f32[2,1,128,128]{2,3,1,0:T(8,128)} custom-call(f32[2,1,128,128]{3,2,1,0:T(8,128)} %get-tuple-element.82), custom_call_target="InvertDiagBlocksLowerTriangular" | custom-call | tf_op jit(solution)/shard_map/jit(cholesky)/cholesky | solution.py:49
  795.5 24.6 %custom-call.78 = f32[2,128,128]{2,1,0:T(8,128)S(1)} custom-call(f32[2,128,128]{2,1,0:T(8,128)} %cholesky.704), custom_call_target="Cholesky" | custom-call | tf_op jit(solution)/shard_map/jit(cholesky)/cholesky | solution.py:49
  820.9 21.1 %custom-call.79 = f32[2,1,128,128]{2,3,1,0:T(8,128)} custom-call(f32[2,1,128,128]{3,2,1,0:T(8,128)} %get-tuple-element.80), custom_call_target="InvertDiagBlocksLowerTriangular" | custom-call | tf_op jit(solution)/shard_map/jit(cholesky)/cholesky | solution.py:49
  846.0 23.5 %custom-call.80 = f32[2,128,128]{2,1,0:T(8,128)S(1)} custom-call(f32[2,128,128]{2,1,0:T(8,128)S(1)} %convolution_subtract_fusion.8), custom_call_target="Cholesky" | custom-call | tf_op jit(solution)/shard_map/jit(cholesky)/cholesky | solution.py:49
  872.1 5.3 select_select_fusion
  878.4 21.5 %while.9 = (s32[]{:T(128)}, f32[2,768,768]{2,1,0:T(8,128)}, s32[6,2]{0,1:T(2,128)S(1)}, f32[6,2,128,128]{3,2,0,1:T(8,128)}, s32[]{:T(128)}) while((s32[]{:T(128)}, f32[2,768,768]{2,1,0:T(8,128)}, s32[6,2]{0,1:T(2,128)S(1)}, f32[6,2,128,128]{3,2,0,1:T(8,128)}, s32[]{:T(128)}) %tuple.98), condition=%wide.while_cond.1.clone, body=%wide.while_body.1.clone.sunk | while | flops 2 | bytes 263777 | solution.py:58
  899.9 119.5 %custom-call.82 = f32[2,6,128,128]{2,3,1,0:T(8,128)} custom-call(f32[2,6,128,128]{3,2,1,0:T(8,128)} %bitcast.492), custom_call_target="InvertDiagBlocksLowerTriangular" | custom-call | tf_op jit(solution)/shard_map/triangular_solve/custom-call.12 | solution.py:58
  1048.9 28.9 %all_gather.3 = f32[2,49152]{1,0:T(2,128)S(1)} all-gather(f32[2,1536]{1,0:T(2,128)S(1)} %pad_maximum_fusion), channel_id=1, replica_groups=mesh['samp'=32,'slab'=4] {'samp'}, dimensions={1}, use_global_device_ids=true | all-gather | bytes 405504 | tf_op jit(solution)/shard_map/all_gather | solution.py:81
  1080.7 3.7 all-to-all-start
  1084.4 4.6 fusion.2
  1094.3 62.8 %psum.30 = f32[3]{0:T(128)} all-reduce(f32[3]{0:T(128)} %maximum_maximum_fusion.1), channel_id=1, replica_groups=mesh['samp'=32,'slab'=4] {'samp'}, use_global_device_ids=true, to_apply=%region_19.23 | all-reduce | flops 3 | bytes 24 | tf_op jit(solution)/shard_map/psum | solution.py:66
  1167.2 9.1 all-reduce.2
  (333 shorter events, 192.8 us)
Async XLA Ops:
  0.6 1165.6 %copy-start = (bf16[128,12288]{1,0:T(8,128)(2,1)S(1)}, bf16[128,12288]{1,0:T(8,128)(2,1)}, u32[]{:S(2)}) copy-start(bf16[128,12288]{1,0:T(8,128)(2,1)} %param.18) | copy-start | bytes 9437188
  0.6 10.0 copy-start.32
  0.7 10.1 copy-start.40
  10.7 11.1 copy-start.13
  11.4 4.3 copy-start.24
  26.2 2.1 copy-start.2
  51.8 27.6 %copy-start.7 = (f32[2,128,128]{2,1,0:T(8,128)}, f32[2,128,128]{2,1,0:T(8,128)S(1)}, u32[]{:S(2)}) copy-start(f32[2,128,128]{2,1,0:T(8,128)S(1)} %custom-call.57) | copy-start | bytes 393220
  78.6 0.8 copy-start.3
  103.1 71.3 %copy-start.9 = (f32[2,128,128]{2,1,0:T(8,128)}, f32[2,128,128]{2,1,0:T(8,128)S(1)}, u32[]{:S(2)}) copy-start(f32[2,128,128]{2,1,0:T(8,128)S(1)} %custom-call.59) | copy-start | bytes 393220
  128.6 0.8 copy-start.5
  152.8 21.7 %copy-start.11 = (f32[2,128,128]{2,1,0:T(8,128)}, f32[2,128,128]{2,1,0:T(8,128)S(1)}, u32[]{:S(2)}) copy-start(f32[2,128,128]{2,1,0:T(8,128)S(1)} %custom-call.61) | copy-start | bytes 393220
  309.1 5.3 copy-start.42
  309.1 147.9 %copy-start.33 = (s32[2]{0:T(128)S(1)}, s32[2]{0:T(128)}, u32[]{:S(2)}) copy-start(s32[2]{0:T(128)} %param.15) | copy-start | bytes 28
  309.1 147.9 %copy-start.36 = (f32[2,768,1]{1,0,2:T(2,128)S(1)}, f32[2,768,1]{1,0,2:T(2,128)}, u32[]{:S(2)}) copy-start(f32[2,768,1]{1,0,2:T(2,128)} %reshape_squeeze.13) | copy-start | bytes 18436
  314.4 157.2 %copy-start.41 = (f32[4]{0:T(128)S(1)}, f32[4]{0:T(128)}, u32[]{:S(2)}) copy-start(f32[4]{0:T(128)} %param.17) | copy-start | bytes 52
  314.4 158.6 %copy-start.37 = (f32[2,1,1536]{2,1,0:T(1,128)S(1)}, f32[2,1,1536]{2,1,0:T(1,128)}, u32[]{:S(2)}) copy-start(f32[2,1,1536]{2,1,0:T(1,128)} %param.14) | copy-start | bytes 36868
  314.4 173.1 %copy-start.14 = (f32[2,768]{1,0:T(2,128)S(1)}, f32[2,768]{1,0:T(2,128)}, u32[]{:S(2)}) copy-start(f32[2,768]{1,0:T(2,128)} %copy-done.13) | copy-start | bytes 18436
  337.5 154.7 %copy-start.16 = (s32[6,2]{0,1:T(2,128)}, s32[6,2]{0,1:T(2,128)S(1)}, u32[]{:S(2)}) copy-start(s32[6,2]{0,1:T(2,128)S(1)} %get-tuple-element.228) | copy-start | bytes 148
  457.1 30.3 %copy-start.29 = (f32[2,768,1]{1,0,2:T(2,128)}, f32[2,768,1]{1,0,2:T(2,128)S(1)}, u32[]{:S(2)}) copy-start(f32[2,768,1]{1,0,2:T(2,128)S(1)} %fusion.130) | copy-start | bytes 18436
  457.1 15.9 %copy-start.38 = (f32[2,128,1]{1,0,2:T(2,128)}, f32[2,128,1]{1,0,2:T(2,128)S(1)}, u32[]{:S(2)}) copy-start(f32[2,128,1]{1,0,2:T(2,128)S(1)} %slice.368) | copy-start | bytes 3076
  463.1 29.1 %copy-start.25 = (f32[2,768]{1,0:T(2,128)S(1)}, f32[2,768]{1,0:T(2,128)}, u32[]{:S(2)}) copy-start(f32[2,768]{1,0:T(2,128)} %copy-done.24) | copy-start | bytes 18436
  463.1 29.1 %copy-start.28 = (f32[2,768]{1,0:T(2,128)S(1)}, f32[2,768]{1,0:T(2,128)}, u32[]{:S(2)}) copy-start(f32[2,768]{1,0:T(2,128)} %reshape_squeeze.15) | copy-start | bytes 18436
  463.1 110.1 %copy-start.31 = (f32[1536]{0:T(1024)S(1)}, f32[1536]{0:T(1024)}, u32[]{:S(2)}) copy-start(f32[1536]{0:T(1024)} %get-tuple-element.97) | copy-start | bytes 18436
  487.5 91.0 %copy-start.18 = (f32[2,768,1]{1,0,2:T(2,128)}, f32[2,768,1]{1,0,2:T(2,128)S(1)}, u32[]{:S(2)}) copy-start(f32[2,768,1]{1,0,2:T(2,128)S(1)} %constant_dynamic-update-slice_fusion.16) | copy-start | bytes 18436
  573.2 5.4 copy-start.22
  573.2 5.3 copy-start.20
  589.0 2.1 copy-start.1
  614.5 27.6 %copy-start.8 = (f32[2,128,128]{2,1,0:T(8,128)}, f32[2,128,128]{2,1,0:T(8,128)S(1)}, u32[]{:S(2)}) copy-start(f32[2,128,128]{2,1,0:T(8,128)S(1)} %custom-call.70) | copy-start | bytes 393220
  641.3 0.8 copy-start.4
  665.8 71.1 %copy-start.10 = (f32[2,128,128]{2,1,0:T(8,128)}, f32[2,128,128]{2,1,0:T(8,128)S(1)}, u32[]{:S(2)}) copy-start(f32[2,128,128]{2,1,0:T(8,128)S(1)} %custom-call.72) | copy-start | bytes 393220
  691.2 0.8 copy-start.6
  715.5 21.5 %copy-start.12 = (f32[2,128,128]{2,1,0:T(8,128)}, f32[2,128,128]{2,1,0:T(8,128)S(1)}, u32[]{:S(2)}) copy-start(f32[2,128,128]{2,1,0:T(8,128)S(1)} %custom-call.74) | copy-start | bytes 393220
  872.0 6.4 copy-start.17
  872.0 147.4 %copy-start.39 = (f32[2,128,1]{1,0,2:T(2,128)S(1)}, f32[2,128,1]{1,0,2:T(2,128)}, u32[]{:S(2)}) copy-start(f32[2,128,1]{1,0,2:T(2,128)} %copy-done.38) | copy-start | bytes 3076
  872.1 149.7 %copy-start.30 = (f32[2,768,1]{1,0,2:T(2,128)S(1)}, f32[2,768,1]{1,0,2:T(2,128)}, u32[]{:S(2)}) copy-start(f32[2,768,1]{1,0,2:T(2,128)} %copy-done.29) | copy-start | bytes 18436
  877.4 156.5 %copy-start.34 = (s32[2]{0:T(128)S(1)}, s32[2]{0:T(128)}, u32[]{:S(2)}) copy-start(s32[2]{0:T(128)} %param.15) | copy-start | bytes 28
  877.4 156.5 %copy-start.35 = (f32[2,768,1]{1,0,2:T(2,128)S(1)}, f32[2,768,1]{1,0,2:T(2,128)}, u32[]{:S(2)}) copy-start(f32[2,768,1]{1,0,2:T(2,128)} %mul.175) | copy-start | bytes 18436
  877.4 170.9 %copy-start.19 = (f32[2,768,1]{1,0,2:T(2,128)S(1)}, f32[2,768,1]{1,0,2:T(2,128)}, u32[]{:S(2)}) copy-start(f32[2,768,1]{1,0,2:T(2,128)} %copy-done.18) | copy-start | bytes 18436
  878.4 206.0 %copy-start.15 = (f32[2,768]{1,0:T(2,128)S(1)}, f32[2,768]{1,0:T(2,128)}, u32[]{:S(2)}) copy-start(f32[2,768]{1,0:T(2,128)} %copy-done.13) | copy-start | bytes 18436
  1048.3 0.6 copy-start.26
  1048.3 0.6 copy-start.27
  1080.7 82.9 %all-to-all-start = ((f32[1,2,32,4,384]{4,2,1,0,3:T(8,128)}), f32[1,2,32,4,384]{4,2,1,0,3:T(8,128)S(1)}, u32[]{:S(2)}, u32[]{:S(2)}) async-start(f32[1,2,32,4,384]{4,2,1,0,3:T(8,128)} %copy.147), calls=%async_computation | async-start | bytes 786432 | tf_op jit(solution)/shard_map/all_to_all | solution.py:83
  1089.0 87.3 %copy-start.21 = (f32[2,768]{1,0:T(2,128)S(1)}, f32[2,768]{1,0:T(2,128)}, u32[]{:S(2)}) copy-start(f32[2,768]{1,0:T(2,128)} %copy-done.20) | copy-start | bytes 18436
  1163.6 12.7 %copy-start.23 = (f32[2,768]{1,0:T(2,128)S(1)}, f32[2,768]{1,0:T(2,128)}, u32[]{:S(2)}) copy-start(f32[2,768]{1,0:T(2,128)} %copy-done.22) | copy-start | bytes 18436
where the time goes:
time: 1190 us; the launch traced here: 1180 us
  other arithmetic  791 us (66%)
  blocking collectives  174 us (15%)
  matrix products  113 us (9%)
  local copies, waits for them, and re-layouts  88.5 us (7%)
    another operation x47, other arithmetic, per_device(): factor = jnp.linalg.cholesky(system)  505 us
    another operation x22, other arithmetic, per_device(): lax.linalg.triangular_solve(factor, forward[:, :, None], left_side=True,...  251 us
    psum x2, blocking collectives, per_device(): totals = lax.psum(stat_row, 'samp')  127 us
    another operation x20, matrix products, per_device(): factor = jnp.linalg.cholesky(system)  46.3 us
    another operation x45, local copies, waits for them, and re-layouts, per_device(): lax.linalg.triangular_solve(factor, forward[:, :, None], left_side=True,...  45.6 us
    all_gather x1, blocking collectives, per_device(): spread = lax.all_gather(stacked, 'samp', axis=1, tiled=True)  28.9 us
    another operation x22, matrix products, per_device(): lax.linalg.triangular_solve(factor, targets[:, :, None], left_side=True,...  28.6 us
    another operation x22, matrix products, per_device(): lax.linalg.triangular_solve(factor, forward[:, :, None], left_side=True,...  28.2 us
  transfers between devices with their start and end apart: 1, of which 0 were waited for; matrix products, arithmetic and copies ran while one was open for 1% of the time, Pallas kernels for 0%

commit v1 on v0

v1 whole, which is shorter than its diff:
```python
import functools

import jax
import jax.numpy as jnp
from jax import lax
from jax.experimental import pallas as pl
from jax.experimental.pallas import tpu as pltpu
from jax.sharding import PartitionSpec as P

SWEEPS = 2
TILE = 128
STEP = 8

shape_total = 1.5
global_shrink = 0.01

MESH = pl.DeviceIdType.MESH
F32 = jnp.float32
BF16 = jnp.bfloat16


def split3(x):
    high = x.astype(BF16)
    rest = x - high.astype(F32)
    mid = rest.astype(BF16)
    low = (rest - mid.astype(F32)).astype(BF16)
    return high, mid, low


def left_terms(x):
    high, mid, low = split3(x)
    return jnp.concatenate([high, high, mid, mid, high, low], axis=1)


def right_terms(x):
    high, mid, low = split3(x)
    return jnp.concatenate([high, mid, high, mid, low, high], axis=0)


def lane_spread(x, column):
    index = jnp.full(x.shape, column, jnp.int32)
    return jnp.take_along_axis(x, index, axis=1, mode="promise_in_bounds")


def row_spread(x, row):
    return jnp.broadcast_to(x[row : row + 1, :], x.shape)


def eliminate(slots, diag, pivots):
    lane = lax.broadcasted_iota(jnp.int32, (STEP, TILE), 1)
    sub = lax.broadcasted_iota(jnp.int32, (STEP, TILE), 0)
    for step in range(TILE // STEP):
        first = step * STEP
        rows = pl.ds(first, STEP)
        value = [diag[b, rows, :] for b in range(slots)]
        columns = [[None] * STEP for _ in range(slots)]
        for j in range(STEP):
            for b in range(slots):
                columns[b][j] = lane_spread(value[b], first + j)
        held = list(value)
        inverse = list(value)
        for j in range(STEP):
            for b in range(slots):
                column = columns[b]
                pivot = 1.0 / row_spread(column[j], j)
                unit = jnp.where(sub == j, 1.0, 0.0)
                v = jnp.where(lane == first + j, unit, value[b])
                held[b] = jnp.where(sub == j, v, held[b])
                inverse[b] = jnp.where(sub == j, pivot, inverse[b])
                factor = jnp.where(sub == j, 0.0, column[j]) * pivot
                value[b] = v - factor * row_spread(v, j)
                for k in range(j + 1, STEP):
                    column[k] = column[k] - factor * row_spread(column[k], j)
        solved = []
        for b in range(slots):
            whole = value[b] * inverse[b]
            diag[b, rows, :] = held[b]
            pivots[b, rows, :] = inverse[b]
            solved.append([row_spread(whole, j) for j in range(STEP)])
        inside = (lane >= first) & (lane < first + STEP)
        later = range(step + 1, TILE // STEP)
        below = {}
        total = {}
        for k in later:
            for b in range(slots):
                below[b, k] = diag[b, pl.ds(k * STEP, STEP), :]
                total[b, k] = jnp.where(inside, 0.0, below[b, k])
        for j in range(STEP):
            for k in later:
                for b in range(slots):
                    total[b, k] = total[b, k] - lane_spread(below[b, k], first + j) * solved[b][j]
        for k in later:
            for b in range(slots):
                diag[b, pl.ds(k * STEP, STEP), :] = total[b, k]


def solve_kernel(slots, size, length, ld, marginal, normals, shrink, noise, effect, stats,
                 work, diag, pivots, rhs, panel):
    tiles = size // TILE
    row = lax.broadcasted_iota(jnp.int32, (TILE, TILE), 0)
    col = lax.broadcasted_iota(jnp.int32, (TILE, TILE), 1)
    wide = lax.broadcasted_iota(jnp.int32, (1, size), 1)
    wide_rows = lax.broadcasted_iota(jnp.int32, (TILE, size), 1)
    noise_level = noise[0:1, 0:1]

    def of_slot(ref, b):
        return ref[0:1, b * size : (b + 1) * size]

    for b in range(slots):
        live = (wide < length[b]).astype(F32)
        extra = live / of_slot(shrink, b) + (1.0 - live)

        def build(r, carry, b=b, live=live, extra=extra):
            rows = pl.ds(pl.multiple_of(r * TILE, TILE), TILE)
            tile_row = lax.broadcasted_iota(jnp.int32, (TILE, 1), 0) + r * TILE
            full_row = lax.broadcasted_iota(jnp.int32, (TILE, size), 0) + r * TILE
            inside = (full_row < length[b]) & (wide_rows < length[b])
            value = jnp.where(inside, ld[b, rows, :].astype(F32), 0.0)
            work[b, rows, :] = value + jnp.where(full_row == wide_rows, extra, 0.0)
            return carry

        lax.fori_loop(0, tiles, build, 0)

    def one_panel(p, totals):
        start = pl.multiple_of(p * TILE, TILE)
        here = pl.ds(start, TILE)
        for b in range(slots):
            diag[b] = work[b, here, here]
        eliminate(slots, diag, pivots)
        result = []
        for b in range(slots):
            lower = jnp.where(col <= row, diag[b], 0.0)
            work[b, here, here] = jnp.where(col == row, 1.0, 0.0)
            rhs[...] = right_terms(work[b, here, :])
            rows = jnp.dot(left_terms(lower), rhs[...], preferred_element_type=F32)
            panel[b] = rows
            inverse = pivots[b]
            inverse_wide = jnp.concatenate([inverse] * tiles, axis=1)
            rhs[...] = right_terms(rows * inverse_wide)

            def below(k, carry, b=b):
                below_rows = pl.ds(pl.multiple_of(k * TILE, TILE), TILE)
                across = panel[b, :, below_rows].T
                change = jnp.dot(left_terms(across), rhs[...], preferred_element_type=F32)
                kept = work[b, below_rows, :]
                gone = (wide_rows >= start) & (wide_rows < start + TILE)
                work[b, below_rows, :] = jnp.where(gone, 0.0, kept) - change
                return carry

            lax.fori_loop(p + 1, tiles, below, 0)
            reach = wide < start + TILE
            live = wide < length[b]
            target = jnp.where(reach & live, of_slot(marginal, b), 0.0)
            forward = jnp.sum(rows * target, axis=1, keepdims=True)
            own = pl.ds(pl.multiple_of(b * size + p * TILE, TILE), TILE)
            own_live = (lax.broadcasted_iota(jnp.int32, (1, TILE), 1) + start) < length[b]
            draw = jnp.where(own_live, normals[0:1, own], 0.0)
            draw = jnp.broadcast_to(draw, (TILE, TILE)).T
            weight = forward * inverse + noise_level * draw * jnp.sqrt(inverse)
            weight_wide = jnp.concatenate([weight] * tiles, axis=1)
            part = jnp.sum(rows * weight_wide, axis=0, keepdims=True)
            result.append(totals[b] + jnp.where(reach, part, 0.0))
        return tuple(result)

    totals = lax.fori_loop(0, tiles, one_panel, tuple(jnp.zeros((1, size), F32) for _ in range(slots)))
    squares = jnp.zeros((1, size), F32)
    count = jnp.zeros((1, size), F32)
    for b in range(slots):
        live = (wide < length[b]).astype(F32)
        value = totals[b] * live
        effect[0:1, b * size : (b + 1) * size] = value
        high, mid, low = split3(value)
        pad = jnp.zeros((5, size), BF16)
        parts = jnp.concatenate([high.astype(F32), mid.astype(F32), low.astype(F32), pad.astype(F32)], axis=0)
        fitted = jnp.dot(parts.astype(BF16), ld[b], preferred_element_type=F32)
        fitted = jnp.sum(fitted, axis=0, keepdims=True)
        misfit = (of_slot(marginal, b) - fitted) * live
        squares = squares + misfit * misfit + value * value * live / of_slot(shrink, b)
        count = count + live
    lane = lax.broadcasted_iota(jnp.int32, (1, TILE), 1)
    stats[...] = jnp.where(lane == 0, jnp.sum(squares), jnp.where(lane == 1, jnp.sum(count), 0.0))


def solve(block_len, ld, marginal, normals, shrink, noise):
    slots, size = ld.shape[0], ld.shape[1]
    vmem = pl.BlockSpec(memory_space=pltpu.VMEM)
    return pl.pallas_call(
        functools.partial(solve_kernel, slots, size),
        out_shape=(
            jax.ShapeDtypeStruct((1, slots * size), F32),
            jax.ShapeDtypeStruct((1, TILE), F32),
        ),
        in_specs=[pl.BlockSpec(memory_space=pltpu.SMEM)] + [vmem] * 5,
        out_specs=(vmem, vmem),
        scratch_shapes=[
            pltpu.VMEM((slots, size, size), F32),
            pltpu.VMEM((slots, TILE, TILE), F32),
            pltpu.VMEM((slots, TILE, TILE), F32),
            pltpu.VMEM((6 * TILE, size), BF16),
            pltpu.VMEM((slots, TILE, size), F32),
        ],
        name="solve",
    )(block_len, ld, marginal, normals, shrink, noise)


def enter(samp, slab, others_samp, others_slab):
    me, my = lax.axis_index("samp"), lax.axis_index("slab")
    barrier = pltpu.get_barrier_semaphore()

    def greet(d, carry):
        peer = lax.rem(me + d, samp)
        pl.semaphore_signal(barrier, inc=1, device_id=(peer, my), device_id_type=MESH)
        return carry

    lax.fori_loop(1, samp, greet, 0)
    for d in range(1, slab):
        peer = lax.rem(my + d, slab)
        pl.semaphore_signal(barrier, inc=1, device_id=(me, peer), device_id_type=MESH)
    pl.semaphore_wait(barrier, samp - 1 + slab - 1)
    return me, my


def sums_of(gathered, slab):
    total = jnp.sum(gathered, axis=0)
    return [total[k : k + 1, :] for k in range(slab)]


def pooled_shrink(totals, effects, weights, shrink, rate):
    pooled = jnp.zeros_like(shrink)
    for k, total in enumerate(totals):
        variance = (total[0:1, 0:1] + 1.0) / (total[0:1, 1:2] + 1.0)
        effect = effects[k]
        pooled = pooled + weights[0:1, k : k + 1] * effect * effect / variance
    new = (pooled + 1.0) / (2.0 + jnp.sqrt(4.0 + 2.0 * rate * (pooled + 1.0)))
    return new


def share_kernel(samp, slab, effect, stats, weights, shrink, new_shrink, noise,
                 effects, own_stats, gathered, e_send, e_recv, s_send, s_recv, g_send, g_recv, local):
    me, my = enter(samp, slab, None, None)
    keep = [
        pltpu.make_async_copy(effect, effects.at[my], local.at[0]),
        pltpu.make_async_copy(stats, own_stats.at[my], local.at[1]),
    ]
    for copy in keep:
        copy.start()
    stat_copies, effect_copies = [], []
    for d in range(1, slab):
        peer = lax.rem(my + d, slab)
        stat_copies.append(pltpu.make_async_remote_copy(
            stats, own_stats.at[my], s_send.at[d], s_recv.at[d], device_id=(me, peer), device_id_type=MESH))
        stat_copies[-1].start()
    for d in range(1, slab):
        peer = lax.rem(my + d, slab)
        effect_copies.append(pltpu.make_async_remote_copy(
            effect, effects.at[my], e_send.at[d], e_recv.at[d], device_id=(me, peer), device_id_type=MESH))
        effect_copies[-1].start()
    for copy in keep:
        copy.wait()
    for copy in stat_copies:
        copy.wait()
    mine = pltpu.make_async_copy(own_stats, gathered.at[me], local.at[0])
    mine.start()

    def spread(d):
        peer = lax.rem(me + d, samp)
        return pltpu.make_async_remote_copy(
            own_stats, gathered.at[me], g_send.at[d], g_recv.at[d], device_id=(peer, my), device_id_type=MESH)

    def start(d, carry):
        spread(d).start()
        return carry

    def finish(d, carry):
        spread(d).wait()
        return carry

    lax.fori_loop(1, samp, start, 0)
    for copy in effect_copies:
        copy.wait()
    lax.fori_loop(1, samp, finish, 0)
    mine.wait()
    totals = sums_of(gathered[:, :, 0, :], slab)
    old = shrink[...]
    rate = shape_total / (old + global_shrink)
    new_shrink[...] = pooled_shrink(totals, [effects[k] for k in range(slab)], weights, old, rate)
    lane = lax.broadcasted_iota(jnp.int32, (1, TILE), 1)
    level = jnp.zeros((1, TILE), F32)
    for k, total in enumerate(totals):
        variance = (total[0:1, 0:1] + 1.0) / (total[0:1, 1:2] + 1.0)
        own = jnp.sqrt(variance / weights[0:1, k : k + 1])
        level = jnp.where(my == k, jnp.broadcast_to(own, (1, TILE)), level)
    noise[...] = level


def share(samp, slab, effect, stats, weights, shrink):
    width = effect.shape[1]
    vmem = pl.BlockSpec(memory_space=pltpu.VMEM)
    dma = pltpu.SemaphoreType.DMA
    return pl.pallas_call(
        functools.partial(share_kernel, samp, slab),
        out_shape=(
            jax.ShapeDtypeStruct((1, width), F32),
            jax.ShapeDtypeStruct((1, TILE), F32),
        ),
        in_specs=[vmem] * 4,
        out_specs=(vmem, vmem),
        scratch_shapes=[
            pltpu.VMEM((slab, 1, width), F32),
            pltpu.VMEM((slab, 1, TILE), F32),
            pltpu.VMEM((samp, slab, 1, TILE), F32),
            dma((slab,)), dma((slab,)), dma((slab,)), dma((slab,)), dma((samp,)), dma((samp,)), dma((2,)),
        ],
        compiler_params=pltpu.CompilerParams(collective_id=0, has_side_effects=True),
        name="share",
    )(effect, stats, weights, shrink)


def finish_kernel(samp, slab, effect, stats, weights, shrink, rate, quarters, dosage, new_shrink, scores,
                  effects, own_stats, gathered, own_quarter, columns, spread_columns, dose, partial, parts,
                  e_send, e_recv, s_send, s_recv, q_send, q_recv, g_send, g_recv, w_send, w_recv,
                  p_send, p_recv, local):
    chunks = quarters.shape[1]
    fetch = pltpu.make_async_copy(dosage, dose, local.at[3])
    fetch.start()
    me, my = enter(samp, slab, None, None)
    keep = [
        pltpu.make_async_copy(effect, effects.at[my], local.at[0]),
        pltpu.make_async_copy(stats, own_stats.at[my], local.at[1]),
        pltpu.make_async_copy(quarters.at[my], own_quarter.at[my], local.at[2]),
    ]
    for copy in keep:
        copy.start()
    first, second = [], []
    for d in range(1, slab):
        peer = lax.rem(my + d, slab)
        to = dict(device_id=(me, peer), device_id_type=MESH)
        first.append(pltpu.make_async_remote_copy(
            quarters.at[peer], own_quarter.at[my], q_send.at[d], q_recv.at[d], **to))
        first[-1].start()
        first.append(pltpu.make_async_remote_copy(stats, own_stats.at[my], s_send.at[d], s_recv.at[d], **to))
        first[-1].start()
    for d in range(1, slab):
        peer = lax.rem(my + d, slab)
        to = dict(device_id=(me, peer), device_id_type=MESH)
        second.append(pltpu.make_async_remote_copy(effect, effects.at[my], e_send.at[d], e_recv.at[d], **to))
        second[-1].start()
    for copy in keep + first:
        copy.wait()
    mine = [
        pltpu.make_async_copy(own_stats, gathered.at[me], local.at[0]),
        pltpu.make_async_copy(own_quarter, columns.at[me], local.at[1]),
    ]
    for copy in mine:
        copy.start()

    def spread(d):
        peer = lax.rem(me + d, samp)
        to = dict(device_id=(peer, my), device_id_type=MESH)
        return (
            pltpu.make_async_remote_copy(own_quarter, columns.at[me], w_send.at[d], w_recv.at[d], **to),
            pltpu.make_async_remote_copy(own_stats, gathered.at[me], g_send.at[d], g_recv.at[d], **to),
        )

    def start(d, carry):
        for copy in spread(d):
            copy.start()
        return carry

    def finish(d, carry):
        for copy in spread(d):
            copy.wait()
        return carry

    lax.fori_loop(1, samp, start, 0)
    for copy in second:
        copy.wait()
    lax.fori_loop(1, samp, finish, 0)
    for copy in mine:
        copy.wait()
    fetch.wait()

    def arrange(g, sums):
        for c in range(chunks):
            value = jnp.concatenate(
                [columns[g, k, pl.ds(c, 1), :] for k in range(slab)] + [jnp.zeros((16 - slab, TILE), F32)], axis=0)
            at = pl.ds(pl.multiple_of((g * chunks + c) * TILE, TILE), TILE)
            value = value.astype(BF16)
            spread_columns[:, at] = value
            sums = sums + value.astype(F32)
        return sums

    sums = lax.fori_loop(0, samp, arrange, jnp.zeros((16, TILE), F32))
    products = lax.dot_general(
        spread_columns[...], dose[...], (((1,), (1,)), ((), ())), preferred_element_type=F32)
    totals = sums_of(gathered[:, :, 0, :], slab)
    part = products - jnp.sum(sums, axis=1, keepdims=True)
    for k in range(slab):
        partial[k] = part[k : k + 1, :]
    last = []
    for d in range(1, slab):
        peer = lax.rem(my + d, slab)
        last.append(pltpu.make_async_remote_copy(
            partial.at[peer], parts.at[my], p_send.at[d], p_recv.at[d], device_id=(me, peer), device_id_type=MESH))
        last[-1].start()
    home = pltpu.make_async_copy(partial.at[my], parts.at[my], local.at[2])
    home.start()
    new_shrink[...] = pooled_shrink(
        totals, [effects[k] for k in range(slab)], weights, shrink[...], rate[...])
    for copy in last:
        copy.wait()
    home.wait()
    total = parts[0]
    for k in range(1, slab):
        total = total + parts[k]
    scores[...] = total / jnp.sqrt(totals[0][0:1, 1:2])


def finish(samp, slab, effect, stats, weights, shrink, rate, quarters, dosage):
    width = effect.shape[1]
    rows = dosage.shape[0]
    vmem = pl.BlockSpec(memory_space=pltpu.VMEM)
    dma = pltpu.SemaphoreType.DMA
    return pl.pallas_call(
        functools.partial(finish_kernel, samp, slab),
        out_shape=(
            jax.ShapeDtypeStruct((1, width), F32),
            jax.ShapeDtypeStruct((1, rows), F32),
        ),
        in_specs=[vmem] * 6 + [pl.BlockSpec(memory_space=pl.ANY)],
        out_specs=(vmem, vmem),
        scratch_shapes=[
            pltpu.VMEM((slab, 1, width), F32),
            pltpu.VMEM((slab, 1, TILE), F32),
            pltpu.VMEM((samp, slab, 1, TILE), F32),
            pltpu.VMEM(quarters.shape, F32),
            pltpu.VMEM((samp, *quarters.shape), F32),
            pltpu.VMEM((16, dosage.shape[1]), BF16),
            pltpu.VMEM(dosage.shape, BF16),
            pltpu.VMEM((slab, 1, rows), F32),
            pltpu.VMEM((slab, 1, rows), F32),
            dma((slab,)), dma((slab,)), dma((slab,)), dma((slab,)), dma((slab,)), dma((slab,)),
            dma((samp,)), dma((samp,)), dma((samp,)), dma((samp,)),
            dma((slab,)), dma((slab,)), dma((4,)),
        ],
        compiler_params=pltpu.CompilerParams(collective_id=1, has_side_effects=True),
        name="finish",
    )(effect, stats, weights, shrink, rate, quarters, dosage)


def per_device(samp, slab, ld_blocks, marginal, normals, block_len, scale_start, ancestry_weight, dosage):
    width = marginal.shape[1]
    own_weight = lax.dynamic_index_in_dim(ancestry_weight, lax.axis_index("slab"), 0, keepdims=False)
    weights = ancestry_weight.reshape(1, slab)
    weights = jnp.pad(weights, ((0, 0), (0, TILE - slab)))
    shrink = scale_start.reshape(1, width)
    noise = jnp.full((1, TILE), jnp.sqrt(1.0 / own_weight), F32)
    effect0, stats0 = solve(block_len, ld_blocks[0], marginal, normals[0], shrink, noise)
    shrink1, noise1 = share(samp, slab, effect0, stats0, weights, shrink)
    effect1, stats1 = solve(block_len, ld_blocks[0], marginal, normals[1], shrink1, noise1)
    effects = (effect0 + effect1) / SWEEPS
    quarters = effects.reshape(slab, width // slab // TILE, TILE)
    rate1 = shape_total / (shrink1 + global_shrink)
    shrink2, scores = finish(samp, slab, effect1, stats1, weights, shrink1, rate1, quarters, dosage)
    return (effects, shrink2.reshape(width), scores.reshape(-1, 1))


def solution(mesh):
    return jax.shard_map(
        functools.partial(per_device, mesh.shape["samp"], mesh.shape["slab"]),
        mesh=mesh,
        in_specs=(
            P("slab", "samp", None, None),
            P("slab", "samp"),
            P(None, "slab", "samp"),
            P("samp"),
            P("samp"),
            P(),
            P("samp", "slab"),
        ),
        out_specs=(P("slab", "samp"), P("samp"), P("samp", "slab")),
        check_vma=False,
    )
```

time: 1190 us -> 140 us (0.12)
  other arithmetic: 791 us -> 3.91 us
  blocking collectives: 174 us -> 0 us
  Pallas kernels: 0 us -> 127 us
  matrix products: 113 us -> 0 us
  local copies, waits for them, and re-layouts: 88.5 us -> 7.24 us
    another operation x87 -> x0, other arithmetic: 761 us -> none  [the longest x47 505 us: per_device(): factor = jnp.linalg.cholesky(system)]
    psum x4 -> x0, blocking collectives: 146 us -> none  [the longest x2 127 us: per_device(): totals = lax.psum(stat_row, 'samp')]
    pallas_call x0 -> x4, Pallas kernels: none -> 127 us  [the longest x2 90.1 us: solve(): pl.pallas_call(functools.partial(solve_kernel, slots, size), out_shape=(j...]
    another operation x64 -> x0, matrix products: 103 us -> none  [the longest x20 46.3 us: per_device(): factor = jnp.linalg.cholesky(system)]
    another operation x64 -> x0, local copies, waits for them, and re-layouts: 54.5 us -> none  [the longest x45 45.6 us: per_device(): lax.linalg.triangular_solve(factor, forward[:, :, None], left_side=True,...]
    all_gather x1 -> x0, blocking collectives: 28.9 us -> none  [per_device(): spread = lax.all_gather(stacked, 'samp', axis=1, tiled=True)]
    unnamed x116 -> x1, local copies, waits for them, and re-layouts: 14 us -> 1.11 us
    add x2 -> x0, local copies, waits for them, and re-layouts: 12.2 us -> none  [per_device(): correlation + identity[None, :, :] * (live_rows * inverse + (1.0 - live_r...]
  transfers between devices with their start and end apart: 1 -> 0, of which waited for: 0 -> 0; matrix products, arithmetic and copies ran while one was open for 1% -> 0% of each run, Pallas kernels for 0% -> 0%
where the time goes in v1:
time: 140 us
  Pallas kernels  127 us (91%)
  local copies, waits for them, and re-layouts  7.24 us (5%)
  other arithmetic  3.91 us (3%)
    pallas_call x2, Pallas kernels, solve(): pl.pallas_call(functools.partial(solve_kernel, slots, size), out_shape=(j...  90.1 us
    pallas_call x1, Pallas kernels, share(): pl.pallas_call(functools.partial(share_kernel, samp, slab), out_shape=(ja...  18.5 us
    pallas_call x1, Pallas kernels, finish(): pl.pallas_call(functools.partial(finish_kernel, samp, slab), out_shape=(j...  18.4 us

profile of v1, /device:TPU:1, one launch (start us, length us, event | category | flops | bytes accessed | tf_op | source)
XLA Modules:
  0.0 139.5 jit_solution(17000527315901652259)
XLA Ops:
  0.6 1.2 dynamic_slice.4
  2.6 0.5 broadcast_in_dim.3.noise
  3.1 1.3 slice_bitcast_fusion
  4.4 1.3 reshape.24.shrink
  5.7 45.1 %solve.2 = (f32[1,1536]{1,0:T(1,128)}, f32[1,128]{1,0:T(1,128)}) custom-call(s32[2]{0:T(128)} %length.3, bf16[2,768,768]{2,1,0:T(8,128)(2,1)} %bitcast.8, f32[1,1536]{1,0:T(1,128)} %marginal.3, f32[1,1536]{1,0:T(1,128)} %get-tuple-element.22.normals, f32[1,1536]{1,0:T(1,128)} %reshape.24.shrink, f32[1,128]{1,0:T(1,128)} %broadcast_in_dim.3.noise), custom_call_target="tpu_custom_call" | custom-call | tf_op jit(solution)/shard_map/solve/pallas_call | solution.py:187
  50.8 1.2 pad.4.weights
  52.0 18.5 %share.1 = (f32[1,1536]{1,0:T(1,128)}, f32[1,128]{1,0:T(1,128)}) custom-call(f32[1,1536]{1,0:T(1,128)} %get-tuple-element.11.effect, f32[1,128]{1,0:T(1,128)} %get-tuple-element.12.stats, f32[1,128]{1,0:T(1,128)} %pad.4.weights, f32[1,1536]{1,0:T(1,128)} %reshape.24.shrink), custom_call_target="tpu_custom_call" | custom-call | tf_op jit(solution)/shard_map/share/pallas_call | solution.py:300
  70.4 45.0 %solve.3 = (f32[1,1536]{1,0:T(1,128)}, f32[1,128]{1,0:T(1,128)}) custom-call(s32[2]{0:T(128)} %length.3, bf16[2,768,768]{2,1,0:T(8,128)(2,1)} %bitcast.9, f32[1,1536]{1,0:T(1,128)} %marginal.3, f32[1,1536]{1,0:T(1,128)} %get-tuple-element.21.normals, f32[1,1536]{1,0:T(1,128)} %get-tuple-element.13.shrink, f32[1,128]{1,0:T(1,128)} %get-tuple-element.14.noise), custom_call_target="tpu_custom_call" | custom-call | tf_op jit(solution)/shard_map/solve/pallas_call | solution.py:187
  115.5 1.3 fusion
  116.8 0.6 reshape.26.quarters
  117.4 1.3 add_divide_fusion.rate
  118.7 18.4 %finish.1 = (f32[1,1536]{1,0:T(1,128)}, f32[1,128]{1,0:T(1,128)}) custom-call(f32[1,1536]{1,0:T(1,128)} %get-tuple-element.15.effect, f32[1,128]{1,0:T(1,128)} %get-tuple-element.16.stats, f32[1,128]{1,0:T(1,128)} %pad.4.weights, f32[1,1536]{1,0:T(1,128)} %get-tuple-element.13.shrink, f32[1,1536]{1,0:T(1,128)} %add_divide_fusion.rate, ...), custom_call_target="tpu_custom_call" | custom-call | tf_op jit(solution)/shard_map/finish/pallas_call | solution.py:424
  137.1 1.3 reduce.1
  138.4 1.1 copy.11

commit v2 on v1

v2 whole, which is shorter than its diff:
```python
import functools

import jax
import jax.numpy as jnp
from jax import lax
from jax.experimental import pallas as pl
from jax.experimental.pallas import tpu as pltpu
from jax.sharding import PartitionSpec as P

SWEEPS = 2
TILE = 128
STEP = 8

shape_total = 1.5
global_shrink = 0.01

MESH = pl.DeviceIdType.MESH
F32 = jnp.float32
BF16 = jnp.bfloat16


def split3(x):
    high = x.astype(BF16)
    rest = x - high.astype(F32)
    mid = rest.astype(BF16)
    low = (rest - mid.astype(F32)).astype(BF16)
    return high, mid, low


def left_terms(x):
    high, mid, low = split3(x)
    return jnp.concatenate([high, high, mid, mid, high, low], axis=1)


def right_terms(x):
    high, mid, low = split3(x)
    return jnp.concatenate([high, mid, high, mid, low, high], axis=0)


def lane_spread(x, column):
    index = jnp.full(x.shape, column, jnp.int32)
    return jnp.take_along_axis(x, index, axis=1, mode="promise_in_bounds")


def row_spread(x, row):
    return jnp.broadcast_to(x[row : row + 1, :], x.shape)


def eliminate(slots, diag, pivots):
    lane = lax.broadcasted_iota(jnp.int32, (STEP, TILE), 1)
    sub = lax.broadcasted_iota(jnp.int32, (STEP, TILE), 0)
    for step in range(TILE // STEP):
        first = step * STEP
        rows = pl.ds(first, STEP)
        value = [diag[b, rows, :] for b in range(slots)]
        columns = [[None] * STEP for _ in range(slots)]
        for j in range(STEP):
            for b in range(slots):
                columns[b][j] = lane_spread(value[b], first + j)
        held = list(value)
        inverse = list(value)
        for j in range(STEP):
            for b in range(slots):
                column = columns[b]
                pivot = 1.0 / row_spread(column[j], j)
                unit = jnp.where(sub == j, 1.0, 0.0)
                v = jnp.where(lane == first + j, unit, value[b])
                held[b] = jnp.where(sub == j, v, held[b])
                inverse[b] = jnp.where(sub == j, pivot, inverse[b])
                factor = jnp.where(sub == j, 0.0, column[j]) * pivot
                value[b] = v - factor * row_spread(v, j)
                for k in range(j + 1, STEP):
                    column[k] = column[k] - factor * row_spread(column[k], j)
        solved = []
        for b in range(slots):
            whole = value[b] * inverse[b]
            diag[b, rows, :] = held[b]
            pivots[b, rows, :] = inverse[b]
            solved.append([row_spread(whole, j) for j in range(STEP)])
        inside = (lane >= first) & (lane < first + STEP)
        later = range(step + 1, TILE // STEP)
        below = {}
        total = {}
        for k in later:
            for b in range(slots):
                below[b, k] = diag[b, pl.ds(k * STEP, STEP), :]
                total[b, k] = jnp.where(inside, 0.0, below[b, k])
        for j in range(STEP):
            for k in later:
                for b in range(slots):
                    total[b, k] = total[b, k] - lane_spread(below[b, k], first + j) * solved[b][j]
        for k in later:
            for b in range(slots):
                diag[b, pl.ds(k * STEP, STEP), :] = total[b, k]


def of_slot(value, b, size):
    return value[0:1, b * size : (b + 1) * size]


def solve(slots, size, length, ld, marginal, normals, shrink, noise_level, work, diag, pivots, rhs, panel):
    tiles = size // TILE
    row = lax.broadcasted_iota(jnp.int32, (TILE, TILE), 0)
    col = lax.broadcasted_iota(jnp.int32, (TILE, TILE), 1)
    wide = lax.broadcasted_iota(jnp.int32, (1, size), 1)
    wide_rows = lax.broadcasted_iota(jnp.int32, (TILE, size), 1)

    for b in range(slots):
        live = (wide < length[b]).astype(F32)
        extra = live / of_slot(shrink, b, size) + (1.0 - live)

        def build(r, carry, b=b, extra=extra):
            rows = pl.ds(pl.multiple_of(r * TILE, TILE), TILE)
            full_row = lax.broadcasted_iota(jnp.int32, (TILE, size), 0) + r * TILE
            inside = (full_row < length[b]) & (wide_rows < length[b])
            value = jnp.where(inside, ld[b, rows, :].astype(F32), 0.0)
            work[b, rows, :] = value + jnp.where(full_row == wide_rows, extra, 0.0)
            return carry

        lax.fori_loop(0, tiles, build, 0)

    def one_panel(p, totals):
        start = pl.multiple_of(p * TILE, TILE)
        here = pl.ds(start, TILE)
        for b in range(slots):
            diag[b] = work[b, here, here]
        eliminate(slots, diag, pivots)
        result = []
        for b in range(slots):
            lower = jnp.where(col <= row, diag[b], 0.0)
            work[b, here, here] = jnp.where(col == row, 1.0, 0.0)
            rhs[...] = right_terms(work[b, here, :])
            rows = jnp.dot(left_terms(lower), rhs[...], preferred_element_type=F32)
            panel[b] = rows
            inverse = pivots[b]
            inverse_wide = jnp.concatenate([inverse] * tiles, axis=1)
            rhs[...] = right_terms(rows * inverse_wide)

            def below(k, carry, b=b):
                below_rows = pl.ds(pl.multiple_of(k * TILE, TILE), TILE)
                across = panel[b, :, below_rows].T
                change = jnp.dot(left_terms(across), rhs[...], preferred_element_type=F32)
                kept = work[b, below_rows, :]
                gone = (wide_rows >= start) & (wide_rows < start + TILE)
                work[b, below_rows, :] = jnp.where(gone, 0.0, kept) - change
                return carry

            lax.fori_loop(p + 1, tiles, below, 0)
            reach = wide < start + TILE
            live = wide < length[b]
            target = jnp.where(reach & live, marginal[0:1, b * size : (b + 1) * size], 0.0)
            forward = jnp.sum(rows * target, axis=1, keepdims=True)
            own = pl.ds(pl.multiple_of(b * size + p * TILE, TILE), TILE)
            own_live = (lax.broadcasted_iota(jnp.int32, (1, TILE), 1) + start) < length[b]
            draw = jnp.where(own_live, normals[0:1, own], 0.0)
            draw = jnp.broadcast_to(draw, (TILE, TILE)).T
            weight = forward * inverse + noise_level * draw * jnp.sqrt(inverse)
            weight_wide = jnp.concatenate([weight] * tiles, axis=1)
            part = jnp.sum(rows * weight_wide, axis=0, keepdims=True)
            result.append(totals[b] + jnp.where(reach, part, 0.0))
        return tuple(result)

    totals = lax.fori_loop(0, tiles, one_panel, tuple(jnp.zeros((1, size), F32) for _ in range(slots)))
    squares = jnp.zeros((1, size), F32)
    count = jnp.zeros((1, size), F32)
    drawn = []
    for b in range(slots):
        live = (wide < length[b]).astype(F32)
        value = totals[b] * live
        drawn.append(value)
        high, mid, low = split3(value)
        parts = jnp.concatenate([high.astype(F32), mid.astype(F32), low.astype(F32), jnp.zeros((5, size), F32)], axis=0)
        fitted = jnp.dot(parts.astype(BF16), ld[b], preferred_element_type=F32)
        fitted = jnp.sum(fitted, axis=0, keepdims=True)
        misfit = (marginal[0:1, b * size : (b + 1) * size] - fitted) * live
        squares = squares + misfit * misfit + value * value * live / of_slot(shrink, b, size)
        count = count + live
    lane = lax.broadcasted_iota(jnp.int32, (1, TILE), 1)
    stats = jnp.where(lane == 0, jnp.sum(squares), jnp.where(lane == 1, jnp.sum(count), 0.0))
    return jnp.concatenate(drawn, axis=1), stats


def variances_of(gathered, slab):
    total = jnp.sum(gathered[:, :, 0, :], axis=0)
    rows = [total[k : k + 1, :] for k in range(slab)]
    return [(r[0:1, 0:1] + 1.0) / (r[0:1, 1:2] + 1.0) for r in rows], rows[0][0:1, 1:2]


def next_shrink(variances, effects, weights, shrink):
    rate = shape_total / (shrink + global_shrink)
    pooled = jnp.zeros_like(shrink)
    for k, variance in enumerate(variances):
        effect = effects[k]
        pooled = pooled + weights[k] * effect * effect / variance
    return (pooled + 1.0) / (2.0 + jnp.sqrt(4.0 + 2.0 * rate * (pooled + 1.0)))


def whole_kernel(samp, slab, slots, size, length, weights_ref, ld, marginal, normals, scale, dosage,
                 mean, new_shrink, scores,
                 work, diag, pivots, rhs, panel, drawn, stats, effects, own_stats, gathered,
                 quarters, columns, spread_columns, dose, partial, parts,
                 e_send, e_recv, s_send, s_recv, g_send, g_recv, q_send, q_recv, w_send, w_recv, p_send, p_recv, local):
    me, my = lax.axis_index("samp"), lax.axis_index("slab")
    width = slots * size
    quarter = width // slab
    barrier = pltpu.get_barrier_semaphore()

    def greet(d, carry):
        pl.semaphore_signal(barrier, inc=1, device_id=(lax.rem(me + d, samp), my), device_id_type=MESH)
        return carry

    lax.fori_loop(1, samp, greet, 0)
    for d in range(1, slab):
        pl.semaphore_signal(barrier, inc=1, device_id=(me, lax.rem(my + d, slab)), device_id_type=MESH)
    fetch = pltpu.make_async_copy(dosage, dose, local.at[0])
    fetch.start()
    weights = [weights_ref[k] for k in range(slab)]
    own_weight = weights[0]
    for k in range(1, slab):
        own_weight = jnp.where(my == k, weights[k], own_weight)
    shrink = scale[...].reshape(1, width)

    def near(d):
        return dict(device_id=(me, lax.rem(my + d, slab)), device_id_type=MESH)

    def far(d):
        return dict(device_id=(lax.rem(me + d, samp), my), device_id_type=MESH)

    def run(copies):
        for copy in copies:
            copy.start()
        return copies

    def wait(copies):
        for copy in copies:
            copy.wait()

    variance = jnp.ones((1, 1), F32)
    for s in range(SWEEPS):
        noise_level = jnp.sqrt(variance / own_weight)
        effect, stat = solve(slots, size, length, ld, marginal, normals.at[s], shrink, noise_level,
                             work, diag, pivots, rhs, panel)
        drawn[s] = effect
        if s == SWEEPS - 1:
            total = drawn[0]
            for r in range(1, SWEEPS):
                total = total + drawn[r]
            mean[...] = total / SWEEPS
        stats[s] = stat
        if s == 0:
            pl.semaphore_wait(barrier, samp - 1 + slab - 1)
        first = [pltpu.make_async_copy(stats.at[s], own_stats.at[s, my], local.at[1])]
        if s == SWEEPS - 1:
            own = pl.ds(pl.multiple_of(my * quarter, TILE), quarter)
            first.append(pltpu.make_async_copy(mean.at[:, own], quarters.at[my], local.at[3]))
        for d in range(1, slab):
            first.append(pltpu.make_async_remote_copy(
                stats.at[s], own_stats.at[s, my], s_send.at[s, d], s_recv.at[s, d], **near(d)))
            if s == SWEEPS - 1:
                theirs = pl.ds(pl.multiple_of(lax.rem(my + d, slab) * quarter, TILE), quarter)
                first.append(pltpu.make_async_remote_copy(
                    mean.at[:, theirs], quarters.at[my], q_send.at[d], q_recv.at[d], **near(d)))
        run(first)
        second = [pltpu.make_async_copy(drawn.at[s], effects.at[s, my], local.at[2])]
        for d in range(1, slab):
            second.append(pltpu.make_async_remote_copy(
                drawn.at[s], effects.at[s, my], e_send.at[s, d], e_recv.at[s, d], **near(d)))
        run(second)
        wait(first)
        mine = [pltpu.make_async_copy(own_stats.at[s], gathered.at[s, me], local.at[1])]
        if s == SWEEPS - 1:
            mine.append(pltpu.make_async_copy(quarters, columns.at[me], local.at[3]))
        run(mine)

        def spread(d, s=s):
            copies = [pltpu.make_async_remote_copy(
                own_stats.at[s], gathered.at[s, me], g_send.at[s, d], g_recv.at[s, d], **far(d))]
            if s == SWEEPS - 1:
                copies.append(pltpu.make_async_remote_copy(
                    quarters, columns.at[me], w_send.at[d], w_recv.at[d], **far(d)))
            return copies

        def start(d, carry, spread=spread):
            run(spread(d))
            return carry

        def finish(d, carry, spread=spread):
            wait(spread(d))
            return carry

        lax.fori_loop(1, samp, start, 0)
        wait(second)
        lax.fori_loop(1, samp, finish, 0)
        wait(mine)
        variances, live_total = variances_of(gathered[s], slab)
        if s < SWEEPS - 1:
            shrink = next_shrink(variances, [effects[s, k] for k in range(slab)], weights, shrink)
            variance = variances[0]
            for k in range(1, slab):
                variance = jnp.where(my == k, variances[k], variance)
    fetch.wait()
    chunks = quarter // TILE

    def arrange(g, sums):
        for c in range(chunks):
            value = jnp.concatenate(
                [columns[g, k, :, pl.ds(c * TILE, TILE)] for k in range(slab)] + [jnp.zeros((16 - slab, TILE), F32)], axis=0)
            at = pl.ds(pl.multiple_of((g * chunks + c) * TILE, TILE), TILE)
            value = value.astype(BF16)
            spread_columns[:, at] = value
            sums = sums + value.astype(F32)
        return sums

    sums = lax.fori_loop(0, samp, arrange, jnp.zeros((16, TILE), F32))
    products = lax.dot_general(
        spread_columns[...], dose[...], (((1,), (1,)), ((), ())), preferred_element_type=F32)
    part = products - jnp.sum(sums, axis=1, keepdims=True)
    for k in range(slab):
        partial[k] = part[k : k + 1, :]
    last = [pltpu.make_async_copy(partial.at[my], parts.at[my], local.at[2])]
    for d in range(1, slab):
        last.append(pltpu.make_async_remote_copy(
            partial.at[lax.rem(my + d, slab)], parts.at[my], p_send.at[d], p_recv.at[d], **near(d)))
    run(last)
    out = next_shrink(variances, [effects[SWEEPS - 1, k] for k in range(slab)], weights, shrink)
    new_shrink[...] = out.reshape(width)
    wait(last)
    total = parts[0]
    for k in range(1, slab):
        total = total + parts[k]
    scores[...] = total / jnp.sqrt(live_total)


def per_device(samp, slab, ld_blocks, marginal, normals, block_len, scale_start, ancestry_weight, dosage):
    slots, size = ld_blocks.shape[1], ld_blocks.shape[2]
    width = slots * size
    rows = dosage.shape[0]
    quarter = width // slab
    vmem = pl.BlockSpec(memory_space=pltpu.VMEM)
    smem = pl.BlockSpec(memory_space=pltpu.SMEM)
    dma = pltpu.SemaphoreType.DMA
    effects, shrink, scores = pl.pallas_call(
        functools.partial(whole_kernel, samp, slab, slots, size),
        out_shape=(
            jax.ShapeDtypeStruct((1, width), F32),
            jax.ShapeDtypeStruct((width,), F32),
            jax.ShapeDtypeStruct((1, rows), F32),
        ),
        in_specs=[smem, smem] + [vmem] * 4 + [pl.BlockSpec(memory_space=pl.ANY)],
        out_specs=(vmem, vmem, vmem),
        scratch_shapes=[
            pltpu.VMEM((slots, size, size), F32),
            pltpu.VMEM((slots, TILE, TILE), F32),
            pltpu.VMEM((slots, TILE, TILE), F32),
            pltpu.VMEM((6 * TILE, size), BF16),
            pltpu.VMEM((slots, TILE, size), F32),
            pltpu.VMEM((SWEEPS, 1, width), F32),
            pltpu.VMEM((SWEEPS, 1, TILE), F32),
            pltpu.VMEM((SWEEPS, slab, 1, width), F32),
            pltpu.VMEM((SWEEPS, slab, 1, TILE), F32),
            pltpu.VMEM((SWEEPS, samp, slab, 1, TILE), F32),
            pltpu.VMEM((slab, 1, quarter), F32),
            pltpu.VMEM((samp, slab, 1, quarter), F32),
            pltpu.VMEM((16, dosage.shape[1]), BF16),
            pltpu.VMEM(dosage.shape, BF16),
            pltpu.VMEM((slab, 1, rows), F32),
            pltpu.VMEM((slab, 1, rows), F32),
            dma((SWEEPS, slab)), dma((SWEEPS, slab)), dma((SWEEPS, slab)), dma((SWEEPS, slab)),
            dma((SWEEPS, samp)), dma((SWEEPS, samp)), dma((slab,)), dma((slab,)), dma((samp,)), dma((samp,)),
            dma((slab,)), dma((slab,)), dma((4,)),
        ],
        compiler_params=pltpu.CompilerParams(collective_id=0, has_side_effects=True),
        name="sweeps",
    )(block_len, ancestry_weight, ld_blocks.reshape(slots, size, size), marginal, normals, scale_start, dosage)
    return (effects, shrink, scores.reshape(rows, 1))


def solution(mesh):
    return jax.shard_map(
        functools.partial(per_device, mesh.shape["samp"], mesh.shape["slab"]),
        mesh=mesh,
        in_specs=(
            P("slab", "samp", None, None),
            P("slab", "samp"),
            P(None, "slab", "samp"),
            P("samp"),
            P("samp"),
            P(),
            P("samp", "slab"),
        ),
        out_specs=(P("slab", "samp"), P("samp"), P("samp", "slab")),
        check_vma=False,
    )
```

time: 140 us -> 122 us (0.87)
  Pallas kernels: 127 us -> 118 us
  other arithmetic: 3.91 us -> 0 us
  local copies, waits for them, and re-layouts: 7.24 us -> 3.76 us
    pallas_call x4 -> x1, Pallas kernels: 127 us -> 118 us  [per_device(): pl.pallas_call(functools.partial(whole_kernel, samp, slab, slots, size),...]
    unnamed x1 -> x3, local copies, waits for them, and re-layouts: 1.11 us -> 3.76 us
    div x2 -> x0, other arithmetic: 2.6 us -> none  [the longest x1 1.31 us: per_device(): effects = (effect0 + effect1) / SWEEPS]
    reshape x2 -> x0, local copies, waits for them, and re-layouts: 1.9 us -> none  [the longest x1 1.29 us: per_device(): shrink = scale_start.reshape(1, width)]
where the time goes in v2:
time: 122 us
  Pallas kernels  118 us (97%)
  local copies, waits for them, and re-layouts  3.76 us (3%)
    pallas_call x1, Pallas kernels, per_device(): pl.pallas_call(functools.partial(whole_kernel, samp, slab, slots, size),...  118 us
    unnamed x3, local copies, waits for them, and re-layouts  3.76 us

profile of v2, /device:TPU:1, one launch (start us, length us, event | category | flops | bytes accessed | tf_op | source)
XLA Modules:
  0.0 122.0 jit_solution(5070804982601001027)
XLA Ops:
  0.6 117.6 %sweeps.1 = (f32[1,1536]{1,0:T(1,128)}, f32[1536]{0:T(1024)}, f32[1,128]{1,0:T(1,128)}) custom-call(s32[2]{0:T(128)} %length.1, f32[4]{0:T(128)} %weights_ref.1, bf16[2,768,768]{2,1,0:T(8,128)(2,1)} %bitcast.2, f32[1,1536]{1,0:T(1,128)} %marginal.1, f32[2,1,1536]{2,1,0:T(1,128)} %normals.1, f32[1536]{0:T(1024)} %scale.1, bf16[128,12288]{1,0:T(8,128)(2,1)} %dosage.1), custom_call_target="tpu_custom_call" | custom-call | tf_op jit(solution)/shard_map/sweeps/pallas_call | solution.py:342
  118.3 1.3 %copy.13 = f32[1,1536]{1,0:T(1,128)} copy(f32[1,1536]{1,0:T(1,128)} %get-tuple-element.12) | data formatting | bytes 12288
  119.5 1.3 %copy.14 = f32[1536]{0:T(1024)} copy(f32[1536]{0:T(1024)} %get-tuple-element.13) | data formatting | bytes 12288
  120.8 1.2 copy.15

commit v3 on v2

v3 whole, which is shorter than its diff:
```python
import functools

import jax
import jax.numpy as jnp
from jax import lax
from jax.experimental import pallas as pl
from jax.experimental.pallas import tpu as pltpu
from jax.sharding import PartitionSpec as P

SWEEPS = 2
TILE = 128
STEP = 8
GROUP = 64
SPREAD = 10
PIECES = 3
LEFT = (0, 0, 1, 1, 0, 2)
RIGHT = (0, 1, 0, 1, 2, 0)

shape_total = 1.5
global_shrink = 0.01

MESH = pl.DeviceIdType.MESH
F32 = jnp.float32
BF16 = jnp.bfloat16


def split3(x):
    high = x.astype(BF16)
    rest = x - high.astype(F32)
    mid = rest.astype(BF16)
    low = (rest - mid.astype(F32)).astype(BF16)
    return high, mid, low


def lane_spread(x, column):
    index = jnp.full(x.shape, column, jnp.int32)
    return jnp.take_along_axis(x, index, axis=1, mode="promise_in_bounds")


def row_spread(x, row):
    return jnp.broadcast_to(x[row : row + 1, :], x.shape)


def eliminate(slots, diag, fillers):
    lane = lax.broadcasted_iota(jnp.int32, (STEP, TILE), 1)
    sub = lax.broadcasted_iota(jnp.int32, (STEP, TILE), 0)
    steps = TILE // STEP
    emitted = 0
    for step in range(steps):
        first = step * STEP
        rows = pl.ds(first, STEP)
        value = [diag[b, rows, :] for b in range(slots)]
        columns = [[None] * STEP for _ in range(slots)]
        for j in range(STEP):
            for b in range(slots):
                columns[b][j] = lane_spread(value[b], first + j)
        held = list(value)
        pivots = list(value)
        for j in range(STEP):
            for b in range(slots):
                column = columns[b]
                pivot = row_spread(column[j], j)
                unit = jnp.where(sub == j, 1.0, 0.0)
                v = jnp.where(lane == first + j, unit, value[b])
                held[b] = jnp.where(sub == j, v, held[b])
                pivots[b] = jnp.where(sub == j, pivot, pivots[b])
                factor = jnp.where(sub == j, 0.0, column[j]) * (1.0 / pivot)
                value[b] = v - factor * row_spread(v, j)
                for k in range(j + 1, STEP):
                    column[k] = column[k] - factor * row_spread(column[k], j)
        later = range(step + 1, (first // GROUP + 1) * GROUP // STEP)
        solved = []
        for b in range(slots):
            root = lax.rsqrt(pivots[b])
            root = root * (1.5 - 0.5 * pivots[b] * root * root)
            diag[b, rows, :] = held[b] * root
            if later:
                whole = value[b] * (1.0 / pivots[b])
                solved.append([row_spread(whole, j) for j in range(STEP)])
        inside = (lane >= first) & (lane < first + STEP)
        below = {}
        total = {}
        for k in later:
            for b in range(slots):
                below[b, k] = diag[b, pl.ds(k * STEP, STEP), :]
                total[b, k] = jnp.where(inside, 0.0, below[b, k])
        for j in range(STEP):
            for k in later:
                for b in range(slots):
                    total[b, k] = total[b, k] - lane_spread(below[b, k], first + j) * solved[b][j]
        for k in later:
            for b in range(slots):
                diag[b, pl.ds(k * STEP, STEP), :] = total[b, k]
        due = min(len(fillers), -(-len(fillers) * (step + 1) // SPREAD))
        while emitted < due:
            fillers[emitted]()
            emitted += 1
        done = first + STEP
        if done % GROUP == 0 and done < TILE:
            group = pl.ds(done - GROUP, GROUP)
            wide = lax.broadcasted_iota(jnp.int32, (TILE - done, TILE), 1)
            gone = (wide >= done - GROUP) & (wide < done)
            group_lane = lax.broadcasted_iota(jnp.int32, (GROUP, TILE), 1)
            group_row = lax.broadcasted_iota(jnp.int32, (GROUP, TILE), 0) + (done - GROUP)
            upper = (group_lane > group_row) & (group_lane < done)
            for b in range(slots):
                pieces = split3(jnp.where(upper, 0.0, diag[b, group, :]))
                left = jnp.concatenate([pieces[i] for i in LEFT], axis=0).T
                right = jnp.concatenate([pieces[i] for i in RIGHT], axis=0)
                change = jnp.dot(left[done:, :], right, preferred_element_type=F32)
                rest = pl.ds(done, TILE - done)
                diag[b, rest, :] = jnp.where(gone, 0.0, diag[b, rest, :]) - change


def of_slot(value, b, size):
    return value[0:1, b * size : (b + 1) * size]


def solve(slots, size, length, ld, marginal, normals, shrink, noise_level,
          work, diag, terms, turned, inverses, forward, draws, residual, blend):
    tiles = size // TILE
    row = lax.broadcasted_iota(jnp.int32, (TILE, TILE), 0)
    col = lax.broadcasted_iota(jnp.int32, (TILE, TILE), 1)
    wide = lax.broadcasted_iota(jnp.int32, (1, size), 1)
    lives = [(wide < length[b]).astype(F32) for b in range(slots)]
    inverse = [lives[b] / of_slot(shrink, b, size) for b in range(slots)]

    def tile(p, count=1):
        return pl.ds(p * TILE, count * TILE)

    def loaded(b, r, c, count):
        across = lax.broadcasted_iota(jnp.int32, (TILE, count * TILE), 1) + c * TILE
        down = lax.broadcasted_iota(jnp.int32, (TILE, count * TILE), 0) + r * TILE
        inside = (down < length[b]) & (across < length[b])
        return jnp.where(inside, ld[b, tile(r), tile(c, count)].astype(F32), 0.0)

    def load_diagonal(b, r):
        at = slice(r * TILE, (r + 1) * TILE)
        extra = inverse[b][:, at] + (1.0 - lives[b][:, at])
        return loaded(b, r, r, 1) + jnp.where(row == col, extra, 0.0)

    def start_up(b):
        residual[b] = marginal[0:1, b * size : (b + 1) * size] * lives[b]
        blend[b] = jnp.zeros((1, size), F32)

    def load_rest(b, r):
        if r > 0:
            work[b, tile(r), tile(r)] = load_diagonal(b, r)
        if r + 1 < tiles:
            work[b, tile(r), tile(r + 1, tiles - r - 1)] = loaded(b, r, r + 1, tiles - r - 1)

    def draw_column(b, p):
        at = slice(p * TILE, (p + 1) * TILE)
        value = normals[0:1, pl.ds(b * size + p * TILE, TILE)] * lives[b][:, at]
        draws[b, p] = jnp.broadcast_to(value, (TILE, TILE)).T

    def make_rows(b, p, c, count):
        pieces = split3(inverses[b, p])
        left = jnp.concatenate([pieces[i] for i in LEFT], axis=1)
        pieces = split3(work[b, tile(p), tile(c, count)])
        right = jnp.concatenate([pieces[i] for i in RIGHT], axis=0)
        rows = jnp.dot(left, right, preferred_element_type=F32)
        work[b, tile(p), tile(c, count)] = rows
        for i, piece in enumerate(split3(rows)[:PIECES]):
            terms[b, p % 2, i, :, tile(c, count)] = piece

    def turn(b, p, k):
        for i in range(PIECES):
            turned[b, p % 2, tile(k), tile(i)] = terms[b, p % 2, i, :, tile(k)].T

    def product(b, p, k, rows, c, count):
        left = jnp.concatenate([turned[b, p % 2, tile(k, rows), tile(i)] for i in LEFT], axis=1)
        right = jnp.concatenate([terms[b, p % 2, i, :, tile(c, count)] for i in RIGHT], axis=0)
        return jnp.dot(left, right, preferred_element_type=F32)

    def trail(b, p, k, rows, c, count):
        work[b, tile(k, rows), tile(c, count)] = work[b, tile(k, rows), tile(c, count)] - product(b, p, k, rows, c, count)

    def step_forward(b, p):
        here = residual[b, :, tile(p)]
        column = jnp.sum(inverses[b, p] * here, axis=1, keepdims=True)
        column = jnp.broadcast_to(column, (TILE, TILE))
        forward[b, p] = column
        normal = draws[b, p]
        upper = jnp.where(col > row, work[b, tile(p), tile(p)], 0.0)
        pivot = jnp.where(col == row, 1.0 / jnp.where(col == row, inverses[b, p], 1.0), 0.0)
        blend[b, :, tile(p)] = blend[b, :, tile(p)] + jnp.sum((upper + pivot) * normal, axis=0, keepdims=True)
        for t in range(p + 1, tiles):
            rows = work[b, tile(p), tile(t)]
            residual[b, :, tile(t)] = residual[b, :, tile(t)] - jnp.sum(rows * column, axis=0, keepdims=True)
            blend[b, :, tile(t)] = blend[b, :, tile(t)] + jnp.sum(rows * normal, axis=0, keepdims=True)

    for b in range(slots):
        diag[b] = load_diagonal(b, 0)
    fillers = [functools.partial(start_up, b) for b in range(slots)]
    for r in range(tiles):
        for b in range(slots):
            fillers.append(functools.partial(load_rest, b, r))
            fillers.append(functools.partial(draw_column, b, r))
    for p in range(tiles):
        eliminate(slots, diag, fillers)
        fillers = []
        for b in range(slots):
            whole = diag[b]
            inverses[b, p] = jnp.where(col <= row, whole, 0.0)
            work[b, tile(p), tile(p)] = whole
        for b in range(slots):
            if p + 1 < tiles:
                make_rows(b, p, p + 1, 1)
                turn(b, p, p + 1)
                diag[b] = work[b, tile(p + 1), tile(p + 1)] - product(b, p, p + 1, 1, p + 1, 1)
        for b in range(slots):
            if p + 2 < tiles:
                fillers.append(functools.partial(make_rows, b, p, p + 2, tiles - p - 2))
        for b in range(slots):
            for k in range(p + 2, tiles):
                fillers.append(functools.partial(turn, b, p, k))
        for c in range(p + 2, tiles, 2):
            count = min(2, tiles - c)
            for b in range(slots):
                fillers.append(functools.partial(trail, b, p, p + 1, c + count - p - 1, c, count))
        for b in range(slots):
            fillers.append(functools.partial(step_forward, b, p))
    for filler in fillers:
        filler()

    solution_rows = [[None] * tiles for _ in range(slots)]
    for p in reversed(range(tiles)):
        for b in range(slots):
            weight = forward[b, p] + noise_level * draws[b, p]
            if p + 1 < tiles:
                known = jnp.zeros((TILE, TILE), F32)
                for t in range(p + 1, tiles):
                    known = known + work[b, tile(p), tile(t)] * solution_rows[b][t]
                weight = weight - jnp.sum(known, axis=1, keepdims=True)
            solution_rows[b][p] = jnp.sum(inverses[b, p] * weight, axis=0, keepdims=True)
    squares = jnp.zeros((1, size), F32)
    count = jnp.zeros((1, size), F32)
    drawn = []
    for b in range(slots):
        value = jnp.concatenate(solution_rows[b], axis=1) * lives[b]
        drawn.append(value)
        pull = inverse[b] * value
        misfit = pull - noise_level * blend[b] * lives[b]
        squares = squares + misfit * misfit + value * pull
        count = count + lives[b]
    lane = lax.broadcasted_iota(jnp.int32, (1, TILE), 1)
    stats = jnp.where(lane == 0, jnp.sum(squares), jnp.where(lane == 1, jnp.sum(count), 0.0))
    return jnp.concatenate(drawn, axis=1), stats


def variances_of(gathered, slab):
    total = jnp.sum(gathered[:, :, 0, :], axis=0)
    rows = [total[k : k + 1, :] for k in range(slab)]
    return [(r[0:1, 0:1] + 1.0) / (r[0:1, 1:2] + 1.0) for r in rows], rows[0][0:1, 1:2]


def next_shrink(variances, effects, weights, shrink):
    rate = shape_total / (shrink + global_shrink)
    pooled = jnp.zeros_like(shrink)
    for k, variance in enumerate(variances):
        effect = effects[k]
        pooled = pooled + weights[k] * effect * effect / variance
    return (pooled + 1.0) / (2.0 + jnp.sqrt(4.0 + 2.0 * rate * (pooled + 1.0)))


def whole_kernel(samp, slab, slots, size, length, weights_ref, ld, marginal, normals, scale, dosage,
                 mean, new_shrink, scores,
                 work, diag, terms, turned, inverses, forward, draws, residual, blend, state, level, drawn, stats, effects, own_stats, gathered,
                 quarters, columns, spread_columns, dose, partial, parts,
                 e_send, e_recv, s_send, s_recv, g_send, g_recv, q_send, q_recv, w_send, w_recv, p_send, p_recv, local):
    me, my = lax.axis_index("samp"), lax.axis_index("slab")
    width = slots * size
    quarter = width // slab
    barrier = pltpu.get_barrier_semaphore()

    def greet(d, carry):
        pl.semaphore_signal(barrier, inc=1, device_id=(lax.rem(me + d, samp), my), device_id_type=MESH)
        return carry

    lax.fori_loop(1, samp, greet, 0)
    for d in range(1, slab):
        pl.semaphore_signal(barrier, inc=1, device_id=(me, lax.rem(my + d, slab)), device_id_type=MESH)
    fetch = pltpu.make_async_copy(dosage, dose, local.at[0])
    fetch.start()
    weights = [weights_ref[k] for k in range(slab)]
    own_weight = weights[0]
    for k in range(1, slab):
        own_weight = jnp.where(my == k, weights[k], own_weight)

    def near(d):
        return dict(device_id=(me, lax.rem(my + d, slab)), device_id_type=MESH)

    def far(d):
        return dict(device_id=(lax.rem(me + d, samp), my), device_id_type=MESH)

    def run(copies):
        for copy in copies:
            copy.start()
        return copies

    def wait(copies):
        for copy in copies:
            copy.wait()

    state[...] = scale[...].reshape(1, width)
    level[...] = jnp.broadcast_to(jnp.sqrt(jnp.ones((1, 1), F32) / own_weight), (1, TILE))

    def near_copies(s):
        return [pltpu.make_async_remote_copy(
            stats.at[s], own_stats.at[s, my], s_send.at[s, d], s_recv.at[s, d], **near(d)) for d in range(1, slab)]

    def quarter_copies():
        copies = []
        for d in range(1, slab):
            theirs = pl.ds(pl.multiple_of(lax.rem(my + d, slab) * quarter, TILE), quarter)
            copies.append(pltpu.make_async_remote_copy(
                mean.at[:, theirs], quarters.at[my], q_send.at[d], q_recv.at[d], **near(d)))
        own = pl.ds(pl.multiple_of(my * quarter, TILE), quarter)
        return copies + [pltpu.make_async_copy(mean.at[:, own], quarters.at[my], local.at[3])]

    def effect_copies(s):
        copies = [pltpu.make_async_remote_copy(
            drawn.at[s], effects.at[s, my], e_send.at[s, d], e_recv.at[s, d], **near(d)) for d in range(1, slab)]
        return copies + [pltpu.make_async_copy(drawn.at[s], effects.at[s, my], local.at[2])]

    def stat_spread(s, d):
        return pltpu.make_async_remote_copy(
            own_stats.at[s], gathered.at[s, me], g_send.at[s, d], g_recv.at[s, d], **far(d))

    def column_spread(d):
        return pltpu.make_async_remote_copy(quarters, columns.at[me], w_send.at[d], w_recv.at[d], **far(d))

    def each(act):
        def one(d, carry):
            act(d)
            return carry

        lax.fori_loop(1, samp, one, 0)

    def sweep(s, carry):
        is_last = s == SWEEPS - 1
        shrink = state[...]
        effect, stat = solve(slots, size, length, ld, marginal, normals.at[s], shrink, level[0:1, 0:1],
                             work, diag, terms, turned, inverses, forward, draws, residual, blend)
        drawn[s] = effect
        stats[s] = stat

        @pl.when(s == 0)
        def _():
            mean[...] = effect
            pl.semaphore_wait(barrier, samp - 1 + slab - 1)

        @pl.when(s > 0)
        def _():
            mean[...] = mean[...] + effect

        @pl.when(is_last)
        def _():
            mean[...] = mean[...] / SWEEPS

        keep = pltpu.make_async_copy(stats.at[s], own_stats.at[s, my], local.at[1])
        run(near_copies(s) + [keep])

        @pl.when(is_last)
        def _():
            run(quarter_copies())

        run(effect_copies(s))
        wait(near_copies(s) + [keep])
        mine = pltpu.make_async_copy(own_stats.at[s], gathered.at[s, me], local.at[1])
        mine.start()
        each(lambda d: stat_spread(s, d).start())

        @pl.when(is_last)
        def _():
            wait(quarter_copies())
            pltpu.make_async_copy(quarters, columns.at[me], local.at[3]).start()
            each(lambda d: column_spread(d).start())

        wait(effect_copies(s))
        each(lambda d: stat_spread(s, d).wait())
        mine.wait()
        variances, _ = variances_of(gathered[s], slab)
        state[...] = next_shrink(variances, [effects[s, k] for k in range(slab)], weights, shrink)
        variance = variances[0]
        for k in range(1, slab):
            variance = jnp.where(my == k, variances[k], variance)
        level[...] = jnp.broadcast_to(jnp.sqrt(variance / own_weight), (1, TILE))
        return carry

    lax.fori_loop(0, SWEEPS, sweep, 0)
    new_shrink[...] = state[...].reshape(width)
    each(lambda d: column_spread(d).wait())
    pltpu.make_async_copy(quarters, columns.at[me], local.at[3]).wait()
    live_total = variances_of(gathered[SWEEPS - 1], slab)[1]
    fetch.wait()
    chunks = quarter // TILE

    def arrange(g, sums):
        for c in range(chunks):
            value = jnp.concatenate(
                [columns[g, k, :, pl.ds(c * TILE, TILE)] for k in range(slab)] + [jnp.zeros((16 - slab, TILE), F32)], axis=0)
            at = pl.ds(pl.multiple_of((g * chunks + c) * TILE, TILE), TILE)
            value = value.astype(BF16)
            spread_columns[:, at] = value
            sums = sums + value.astype(F32)
        return sums

    sums = lax.fori_loop(0, samp, arrange, jnp.zeros((16, TILE), F32))
    products = lax.dot_general(
        spread_columns[...], dose[...], (((1,), (1,)), ((), ())), preferred_element_type=F32)
    part = products - jnp.sum(sums, axis=1, keepdims=True)
    for k in range(slab):
        partial[k] = part[k : k + 1, :]
    last = [pltpu.make_async_copy(partial.at[my], parts.at[my], local.at[2])]
    for d in range(1, slab):
        last.append(pltpu.make_async_remote_copy(
            partial.at[lax.rem(my + d, slab)], parts.at[my], p_send.at[d], p_recv.at[d], **near(d)))
    run(last)
    wait(last)
    total = parts[0]
    for k in range(1, slab):
        total = total + parts[k]
    scores[...] = total / jnp.sqrt(live_total)


def per_device(samp, slab, ld_blocks, marginal, normals, block_len, scale_start, ancestry_weight, dosage):
    slots, size = ld_blocks.shape[1], ld_blocks.shape[2]
    width = slots * size
    rows = dosage.shape[0]
    quarter = width // slab
    vmem = pl.BlockSpec(memory_space=pltpu.VMEM)
    smem = pl.BlockSpec(memory_space=pltpu.SMEM)
    dma = pltpu.SemaphoreType.DMA
    effects, shrink, scores = pl.pallas_call(
        functools.partial(whole_kernel, samp, slab, slots, size),
        out_shape=(
            jax.ShapeDtypeStruct((1, width), F32),
            jax.ShapeDtypeStruct((width,), F32),
            jax.ShapeDtypeStruct((1, rows), F32),
        ),
        in_specs=[smem, smem] + [vmem] * 4 + [pl.BlockSpec(memory_space=pl.ANY)],
        out_specs=(vmem, vmem, vmem),
        scratch_shapes=[
            pltpu.VMEM((slots, size, size), F32),
            pltpu.VMEM((slots, TILE, TILE), F32),
            pltpu.VMEM((slots, 2, PIECES, TILE, size), BF16),
            pltpu.VMEM((slots, 2, size, PIECES * TILE), BF16),
            pltpu.VMEM((slots, size // TILE, TILE, TILE), F32),
            pltpu.VMEM((slots, size // TILE, TILE, TILE), F32),
            pltpu.VMEM((slots, size // TILE, TILE, TILE), F32),
            pltpu.VMEM((slots, 1, size), F32),
            pltpu.VMEM((slots, 1, size), F32),
            pltpu.VMEM((1, width), F32),
            pltpu.VMEM((1, TILE), F32),
            pltpu.VMEM((SWEEPS, 1, width), F32),
            pltpu.VMEM((SWEEPS, 1, TILE), F32),
            pltpu.VMEM((SWEEPS, slab, 1, width), F32),
            pltpu.VMEM((SWEEPS, slab, 1, TILE), F32),
            pltpu.VMEM((SWEEPS, samp, slab, 1, TILE), F32),
            pltpu.VMEM((slab, 1, quarter), F32),
            pltpu.VMEM((samp, slab, 1, quarter), F32),
            pltpu.VMEM((16, dosage.shape[1]), BF16),
            pltpu.VMEM(dosage.shape, BF16),
            pltpu.VMEM((slab, 1, rows), F32),
            pltpu.VMEM((slab, 1, rows), F32),
            dma((SWEEPS, slab)), dma((SWEEPS, slab)), dma((SWEEPS, slab)), dma((SWEEPS, slab)),
            dma((SWEEPS, samp)), dma((SWEEPS, samp)), dma((slab,)), dma((slab,)), dma((samp,)), dma((samp,)),
            dma((slab,)), dma((slab,)), dma((4,)),
        ],
        compiler_params=pltpu.CompilerParams(collective_id=0, has_side_effects=True),
        name="sweeps",
    )(block_len, ancestry_weight, ld_blocks.reshape(slots, size, size), marginal, normals, scale_start, dosage)
    return (effects, shrink, scores.reshape(rows, 1))


def solution(mesh):
    return jax.shard_map(
        functools.partial(per_device, mesh.shape["samp"], mesh.shape["slab"]),
        mesh=mesh,
        in_specs=(
            P("slab", "samp", None, None),
            P("slab", "samp"),
            P(None, "slab", "samp"),
            P("samp"),
            P("samp"),
            P(),
            P("samp", "slab"),
        ),
        out_specs=(P("slab", "samp"), P("samp"), P("samp", "slab")),
        check_vma=False,
    )
```

time: 122 us -> 86.6 us (0.71)
  Pallas kernels: 118 us -> 81.9 us
    pallas_call x1, Pallas kernels: 118 us -> 81.9 us  [per_device(): pl.pallas_call(functools.partial(whole_kernel, samp, slab, slots, size),...]
where the time goes in v3:
time: 86.6 us; the launch traced here: 86.3 us
  Pallas kernels  81.9 us (95%)
  local copies, waits for them, and re-layouts  3.76 us (4%)
    pallas_call x1, Pallas kernels, per_device(): pl.pallas_call(functools.partial(whole_kernel, samp, slab, slots, size),...  81.9 us
    unnamed x3, local copies, waits for them, and re-layouts  3.76 us

profile of v3, /device:TPU:1, one launch (start us, length us, event | category | flops | bytes accessed | tf_op | source)
XLA Modules:
  0.0 86.3 jit_solution(3996250813881405985)
XLA Ops:
  0.6 81.9 %sweeps.1 = (f32[1,1536]{1,0:T(1,128)}, f32[1536]{0:T(1024)}, f32[1,128]{1,0:T(1,128)}) custom-call(s32[2]{0:T(128)} %length.1, f32[4]{0:T(128)} %weights_ref.1, bf16[2,768,768]{2,1,0:T(8,128)(2,1)} %bitcast.2, f32[1,1536]{1,0:T(1,128)} %marginal.1, f32[2,1,1536]{2,1,0:T(1,128)} %normals.1, f32[1536]{0:T(1024)} %scale.1, bf16[128,12288]{1,0:T(8,128)(2,1)} %dosage.1), custom_call_target="tpu_custom_call" | custom-call | tf_op jit(solution)/shard_map/sweeps/pallas_call | solution.py:436
  82.6 1.3 %copy.13 = f32[1,1536]{1,0:T(1,128)} copy(f32[1,1536]{1,0:T(1,128)} %get-tuple-element.12) | data formatting | bytes 12288
  83.9 1.3 %copy.14 = f32[1536]{0:T(1024)} copy(f32[1536]{0:T(1024)} %get-tuple-element.13) | data formatting | bytes 12288
  85.2 1.2 %copy.15 = f32[128,1]{0,1:T(1,128)} copy(f32[128,1]{0,1:T(1,128)} %bitcast.3) | data formatting | bytes 1024

commit v4 on v3

--- a/solution.py
+++ b/solution.py
@@ -56,18 +56,33 @@
                 columns[b][j] = lane_spread(value[b], first + j)
         held = list(value)
         pivots = list(value)
-        for j in range(STEP):
+        straight = list(value)
+        crossed = list(value)
+        for j in range(0, STEP, 2):
+            pair = (sub == j) | (sub == j + 1)
             for b in range(slots):
                 column = columns[b]
-                pivot = row_spread(column[j], j)
-                unit = jnp.where(sub == j, 1.0, 0.0)
-                v = jnp.where(lane == first + j, unit, value[b])
+                left, right = column[j], column[j + 1]
+                one = row_spread(left, j)
+                two = row_spread(right, j + 1)
+                mixed = row_spread(right, j)
+                scale = 1.0 / (one * two - mixed * mixed)
+                left = jnp.where(pair, 0.0, left)
+                right = jnp.where(pair, 0.0, right)
+                factor = (left * two - right * mixed) * scale
+                second = (right * one - left * mixed) * scale
+                for k in range(j + 2, STEP):
+                    column[k] = (column[k] - factor * row_spread(column[k], j)) - second * row_spread(column[k], j + 1)
+                slope = mixed * (1.0 / one)
+                v = jnp.where(lane == first + j, jnp.where(sub == j, 1.0, 0.0), value[b])
                 held[b] = jnp.where(sub == j, v, held[b])
-                pivots[b] = jnp.where(sub == j, pivot, pivots[b])
-                factor = jnp.where(sub == j, 0.0, column[j]) * (1.0 / pivot)
-                value[b] = v - factor * row_spread(v, j)
-                for k in range(j + 1, STEP):
-                    column[k] = column[k] - factor * row_spread(column[k], j)
+                v = jnp.where(lane == first + j + 1, jnp.where(sub == j + 1, 1.0, 0.0), v)
+                upper = row_spread(v, j)
+                held[b] = jnp.where(sub == j + 1, v - slope * upper, held[b])
+                pivots[b] = jnp.where(sub == j, one, jnp.where(sub == j + 1, two - mixed * slope, pivots[b]))
+                straight[b] = jnp.where(sub == j, two * scale, jnp.where(sub == j + 1, one * scale, straight[b]))
+                crossed[b] = jnp.where(pair, mixed * scale, crossed[b])
+                value[b] = (v - factor * upper) - second * row_spread(v, j + 1)
         later = range(step + 1, (first // GROUP + 1) * GROUP // STEP)
         solved = []
         for b in range(slots):
@@ -75,7 +90,8 @@
             root = root * (1.5 - 0.5 * pivots[b] * root * root)
             diag[b, rows, :] = held[b] * root
             if later:
-                whole = value[b] * (1.0 / pivots[b])
+                swapped = jnp.where(sub % 2 == 0, pltpu.roll(value[b], STEP - 1, 0), pltpu.roll(value[b], 1, 0))
+                whole = value[b] * straight[b] - swapped * crossed[b]
                 solved.append([row_spread(whole, j) for j in range(STEP)])
         inside = (lane >= first) & (lane < first + STEP)
         below = {}
@@ -84,10 +100,12 @@
             for b in range(slots):
                 below[b, k] = diag[b, pl.ds(k * STEP, STEP), :]
                 total[b, k] = jnp.where(inside, 0.0, below[b, k])
-        for j in range(STEP):
-            for k in later:
-                for b in range(slots):
-                    total[b, k] = total[b, k] - lane_spread(below[b, k], first + j) * solved[b][j]
+        for k in later:
+            for b in range(slots):
+                parts = [lane_spread(below[b, k], first + j) * solved[b][j] for j in range(STEP)]
+                while len(parts) > 1:
+                    parts = [parts[i] + parts[i + 1] for i in range(0, len(parts), 2)]
+                total[b, k] = total[b, k] - parts[0]
         for k in later:
             for b in range(slots):
                 diag[b, pl.ds(k * STEP, STEP), :] = total[b, k]
@@ -250,8 +268,11 @@
 
 
 def variances_of(gathered, slab):
-    total = jnp.sum(gathered[:, :, 0, :], axis=0)
-    rows = [total[k : k + 1, :] for k in range(slab)]
+    total = jnp.sum(gathered.reshape(-1, 8, TILE), axis=0)
+    rows = []
+    for k in range(slab):
+        parts = [total[r : r + 1, :] for r in range(k, 8, slab)]
+        rows.append(sum(parts[1:], parts[0]))
     return [(r[0:1, 0:1] + 1.0) / (r[0:1, 1:2] + 1.0) for r in rows], rows[0][0:1, 1:2]
 
 
@@ -266,21 +287,28 @@
 
 def whole_kernel(samp, slab, slots, size, length, weights_ref, ld, marginal, normals, scale, dosage,
                  mean, new_shrink, scores,
-                 work, diag, terms, turned, inverses, forward, draws, residual, blend, state, level, drawn, stats, effects, own_stats, gathered,
-                 quarters, columns, spread_columns, dose, partial, parts,
-                 e_send, e_recv, s_send, s_recv, g_send, g_recv, q_send, q_recv, w_send, w_recv, p_send, p_recv, local):
+                 work, diag, terms, turned, inverses, forward, draws, residual, blend, state, level, drawn, stats, effects, gathered, columns, spread_columns, dose, partial, parts,
+                 e_send, e_recv, g_send, g_recv, w_send, w_recv, p_send, p_recv, local):
     me, my = lax.axis_index("samp"), lax.axis_index("slab")
     width = slots * size
     quarter = width // slab
     barrier = pltpu.get_barrier_semaphore()
 
+    everyone = samp * slab
+    own = me * slab + my
+
+    def peer_of(d):
+        peer = lax.rem(own + d, everyone)
+        return lax.div(peer, slab), lax.rem(peer, slab)
+
+    def far_first(d):
+        return lax.rem(d + everyone // 2 - 2, everyone - 1) + 1
+
     def greet(d, carry):
-        pl.semaphore_signal(barrier, inc=1, device_id=(lax.rem(me + d, samp), my), device_id_type=MESH)
+        pl.semaphore_signal(barrier, inc=1, device_id=peer_of(d), device_id_type=MESH)
         return carry
 
-    lax.fori_loop(1, samp, greet, 0)
-    for d in range(1, slab):
-        pl.semaphore_signal(barrier, inc=1, device_id=(me, lax.rem(my + d, slab)), device_id_type=MESH)
+    lax.fori_loop(1, everyone, greet, 0)
     fetch = pltpu.make_async_copy(dosage, dose, local.at[0])
     fetch.start()
     weights = [weights_ref[k] for k in range(slab)]
@@ -291,9 +319,6 @@
     def near(d):
         return dict(device_id=(me, lax.rem(my + d, slab)), device_id_type=MESH)
 
-    def far(d):
-        return dict(device_id=(lax.rem(me + d, samp), my), device_id_type=MESH)
-
     def run(copies):
         for copy in copies:
             copy.start()
@@ -306,19 +331,6 @@
     state[...] = scale[...].reshape(1, width)
     level[...] = jnp.broadcast_to(jnp.sqrt(jnp.ones((1, 1), F32) / own_weight), (1, TILE))
 
-    def near_copies(s):
-        return [pltpu.make_async_remote_copy(
-            stats.at[s], own_stats.at[s, my], s_send.at[s, d], s_recv.at[s, d], **near(d)) for d in range(1, slab)]
-
-    def quarter_copies():
-        copies = []
-        for d in range(1, slab):
-            theirs = pl.ds(pl.multiple_of(lax.rem(my + d, slab) * quarter, TILE), quarter)
-            copies.append(pltpu.make_async_remote_copy(
-                mean.at[:, theirs], quarters.at[my], q_send.at[d], q_recv.at[d], **near(d)))
-        own = pl.ds(pl.multiple_of(my * quarter, TILE), quarter)
-        return copies + [pltpu.make_async_copy(mean.at[:, own], quarters.at[my], local.at[3])]
-
     def effect_copies(s):
         copies = [pltpu.make_async_remote_copy(
             drawn.at[s], effects.at[s, my], e_send.at[s, d], e_recv.at[s, d], **near(d)) for d in range(1, slab)]
@@ -326,17 +338,24 @@
 
     def stat_spread(s, d):
         return pltpu.make_async_remote_copy(
-            own_stats.at[s], gathered.at[s, me], g_send.at[s, d], g_recv.at[s, d], **far(d))
+            stats.at[s], gathered.at[s, pl.ds(own, 1), :], g_send.at[s], g_recv.at[s],
+            device_id=peer_of(d), device_id_type=MESH)
+
+    def quarter_of(k):
+        return mean.at[:, pl.ds(pl.multiple_of(k * quarter, TILE), quarter)]
 
     def column_spread(d):
-        return pltpu.make_async_remote_copy(quarters, columns.at[me], w_send.at[d], w_recv.at[d], **far(d))
+        peer = peer_of(d)
+        return pltpu.make_async_remote_copy(
+            quarter_of(peer[1]), columns.at[me, my], w_send.at[0], w_recv.at[0],
+            device_id=peer, device_id_type=MESH)
 
     def each(act):
         def one(d, carry):
-            act(d)
+            act(far_first(d))
             return carry
 
-        lax.fori_loop(1, samp, one, 0)
+        lax.fori_loop(1, everyone, one, 0, unroll=4)
 
     def sweep(s, carry):
         is_last = s == SWEEPS - 1
@@ -349,7 +368,7 @@
         @pl.when(s == 0)
         def _():
             mean[...] = effect
-            pl.semaphore_wait(barrier, samp - 1 + slab - 1)
+            pl.semaphore_wait(barrier, everyone - 1)
 
         @pl.when(s > 0)
         def _():
@@ -359,28 +378,17 @@
         def _():
             mean[...] = mean[...] / SWEEPS
 
-        keep = pltpu.make_async_copy(stats.at[s], own_stats.at[s, my], local.at[1])
-        run(near_copies(s) + [keep])
+        each(lambda d: stat_spread(s, d).start())
+        pltpu.make_async_copy(stats.at[s], gathered.at[s, pl.ds(own, 1), :], g_recv.at[s]).start()
+        run(effect_copies(s))
 
         @pl.when(is_last)
         def _():
-            run(quarter_copies())
-
-        run(effect_copies(s))
-        wait(near_copies(s) + [keep])
-        mine = pltpu.make_async_copy(own_stats.at[s], gathered.at[s, me], local.at[1])
-        mine.start()
-        each(lambda d: stat_spread(s, d).start())
-
-        @pl.when(is_last)
-        def _():
-            wait(quarter_copies())
-            pltpu.make_async_copy(quarters, columns.at[me], local.at[3]).start()
             each(lambda d: column_spread(d).start())
+            pltpu.make_async_copy(quarter_of(my), columns.at[me, my], w_recv.at[0]).start()
 
         wait(effect_copies(s))
-        each(lambda d: stat_spread(s, d).wait())
-        mine.wait()
+        pltpu.make_async_copy(gathered.at[s], gathered.at[s], g_recv.at[s]).wait()
         variances, _ = variances_of(gathered[s], slab)
         state[...] = next_shrink(variances, [effects[s, k] for k in range(slab)], weights, shrink)
         variance = variances[0]
@@ -391,8 +399,7 @@
 
     lax.fori_loop(0, SWEEPS, sweep, 0)
     new_shrink[...] = state[...].reshape(width)
-    each(lambda d: column_spread(d).wait())
-    pltpu.make_async_copy(quarters, columns.at[me], local.at[3]).wait()
+    pltpu.make_async_copy(columns, columns, w_recv.at[0]).wait()
     live_total = variances_of(gathered[SWEEPS - 1], slab)[1]
     fetch.wait()
     chunks = quarter // TILE
@@ -419,10 +426,25 @@
             partial.at[lax.rem(my + d, slab)], parts.at[my], p_send.at[d], p_recv.at[d], **near(d)))
     run(last)
     wait(last)
+    for s in range(SWEEPS):
+        sent = gathered.at[s, pl.ds(0, everyone - 1), :]
+        pltpu.make_async_copy(sent, sent, g_send.at[s]).wait()
+
+    def drain(d, carry):
+        pltpu.make_async_copy(columns.at[0, 0], columns.at[0, 0], w_send.at[0]).wait()
+        return carry
+
+    lax.fori_loop(1, everyone, drain, 0)
     total = parts[0]
     for k in range(1, slab):
         total = total + parts[k]
     scores[...] = total / jnp.sqrt(live_total)
+
+
+def hand_over(effects, shrink, scores, effects_out, shrink_out, scores_out):
+    effects_out[...] = effects[...]
+    shrink_out[...] = shrink[...]
+    scores_out[...] = scores[...]
 
 
 def per_device(samp, slab, ld_blocks, marginal, normals, block_len, scale_start, ancestry_weight, dosage):
@@ -457,21 +479,29 @@
             pltpu.VMEM((SWEEPS, 1, width), F32),
             pltpu.VMEM((SWEEPS, 1, TILE), F32),
             pltpu.VMEM((SWEEPS, slab, 1, width), F32),
-            pltpu.VMEM((SWEEPS, slab, 1, TILE), F32),
-            pltpu.VMEM((SWEEPS, samp, slab, 1, TILE), F32),
-            pltpu.VMEM((slab, 1, quarter), F32),
+            pltpu.VMEM((SWEEPS, samp * slab, TILE), F32),
             pltpu.VMEM((samp, slab, 1, quarter), F32),
             pltpu.VMEM((16, dosage.shape[1]), BF16),
             pltpu.VMEM(dosage.shape, BF16),
             pltpu.VMEM((slab, 1, rows), F32),
             pltpu.VMEM((slab, 1, rows), F32),
-            dma((SWEEPS, slab)), dma((SWEEPS, slab)), dma((SWEEPS, slab)), dma((SWEEPS, slab)),
-            dma((SWEEPS, samp)), dma((SWEEPS, samp)), dma((slab,)), dma((slab,)), dma((samp,)), dma((samp,)),
+            dma((SWEEPS, slab)), dma((SWEEPS, slab)), dma((SWEEPS,)), dma((SWEEPS,)), dma((1,)), dma((1,)),
             dma((slab,)), dma((slab,)), dma((4,)),
         ],
         compiler_params=pltpu.CompilerParams(collective_id=0, has_side_effects=True),
         name="sweeps",
     )(block_len, ancestry_weight, ld_blocks.reshape(slots, size, size), marginal, normals, scale_start, dosage)
+    effects, shrink, scores = pl.pallas_call(
+        hand_over,
+        out_shape=(
+            jax.ShapeDtypeStruct((1, width), F32),
+            jax.ShapeDtypeStruct((width,), F32),
+            jax.ShapeDtypeStruct((1, rows), F32),
+        ),
+        in_specs=[vmem] * 3,
+        out_specs=(vmem,) * 3,
+        name="hand_over",
+    )(effects, shrink, scores)
     return (effects, shrink, scores.reshape(rows, 1))
 
 

time: 86.6 us -> 77.1 us (0.89)
  Pallas kernels: 81.9 us -> 76.3 us
  local copies, waits for them, and re-layouts: 3.76 us -> 0 us
    pallas_call x1, Pallas kernels: 81.9 us -> 75 us  [per_device(): pl.pallas_call(functools.partial(whole_kernel, samp, slab, slots, size),...]
    unnamed x3 -> x0, local copies, waits for them, and re-layouts: 3.76 us -> none
    pallas_call x0 -> x1, Pallas kernels: none -> 1.31 us  [per_device(): pl.pallas_call(hand_over, out_shape=(jax.ShapeDtypeStruct((1, width), F32...]
where the time goes in v4:
time: 77.1 us; the launch traced here: 76.9 us
  Pallas kernels  76.3 us (99%)
    pallas_call x1, Pallas kernels, per_device(): pl.pallas_call(functools.partial(whole_kernel, samp, slab, slots, size),...  75 us

profile of v4, /device:TPU:1, one launch (start us, length us, event | category | flops | bytes accessed | tf_op | source)
XLA Modules:
  0.0 76.9 jit_solution(16204073791869471963)
XLA Ops:
  0.6 75.0 %sweeps.1 = (f32[1,1536]{1,0:T(1,128)}, f32[1536]{0:T(1024)}, f32[1,128]{1,0:T(1,128)}) custom-call(s32[2]{0:T(128)} %length.1, f32[4]{0:T(128)} %weights_ref.1, bf16[2,768,768]{2,1,0:T(8,128)(2,1)} %bitcast.2, f32[1,1536]{1,0:T(1,128)} %marginal.1, f32[2,1,1536]{2,1,0:T(1,128)} %normals.1, f32[1536]{0:T(1024)} %scale.1, bf16[128,12288]{1,0:T(8,128)(2,1)} %dosage.1), custom_call_target="tpu_custom_call" | custom-call | tf_op jit(solution)/shard_map/sweeps/pallas_call | solution.py:458
  75.6 1.3 %hand_over.1 = (f32[1,1536]{1,0:T(1,128)}, f32[1536]{0:T(1024)}, f32[1,128]{1,0:T(1,128)}) custom-call(f32[1,1536]{1,0:T(1,128)} %get-tuple-element.9.effects, f32[1536]{0:T(1024)} %get-tuple-element.10.shrink, f32[1,128]{1,0:T(1,128)} %get-tuple-element.11.scores), custom_call_target="tpu_custom_call" | custom-call | tf_op jit(solution)/shard_map/hand_over/pallas_call | solution.py:494

commit v5 on v4

--- a/solution.py
+++ b/solution.py
@@ -252,19 +252,20 @@
                     known = known + work[b, tile(p), tile(t)] * solution_rows[b][t]
                 weight = weight - jnp.sum(known, axis=1, keepdims=True)
             solution_rows[b][p] = jnp.sum(inverses[b, p] * weight, axis=0, keepdims=True)
-    squares = jnp.zeros((1, size), F32)
-    count = jnp.zeros((1, size), F32)
-    drawn = []
-    for b in range(slots):
-        value = jnp.concatenate(solution_rows[b], axis=1) * lives[b]
-        drawn.append(value)
-        pull = inverse[b] * value
-        misfit = pull - noise_level * blend[b] * lives[b]
-        squares = squares + misfit * misfit + value * pull
-        count = count + lives[b]
-    lane = lax.broadcasted_iota(jnp.int32, (1, TILE), 1)
-    stats = jnp.where(lane == 0, jnp.sum(squares), jnp.where(lane == 1, jnp.sum(count), 0.0))
-    return jnp.concatenate(drawn, axis=1), stats
+    drawn = [jnp.concatenate(solution_rows[b], axis=1) * lives[b] for b in range(slots)]
+
+    def totals():
+        squares = jnp.zeros((1, size), F32)
+        count = jnp.zeros((1, size), F32)
+        for b in range(slots):
+            pull = inverse[b] * drawn[b]
+            misfit = pull - noise_level * blend[b] * lives[b]
+            squares = squares + misfit * misfit + drawn[b] * pull
+            count = count + lives[b]
+        lane = lax.broadcasted_iota(jnp.int32, (1, TILE), 1)
+        return jnp.where(lane == 0, jnp.sum(squares), jnp.where(lane == 1, jnp.sum(count), 0.0))
+
+    return jnp.concatenate(drawn, axis=1), totals
 
 
 def variances_of(gathered, slab):
@@ -360,10 +361,9 @@
     def sweep(s, carry):
         is_last = s == SWEEPS - 1
         shrink = state[...]
-        effect, stat = solve(slots, size, length, ld, marginal, normals.at[s], shrink, level[0:1, 0:1],
-                             work, diag, terms, turned, inverses, forward, draws, residual, blend)
+        effect, totals = solve(slots, size, length, ld, marginal, normals.at[s], shrink, level[0:1, 0:1],
+                               work, diag, terms, turned, inverses, forward, draws, residual, blend)
         drawn[s] = effect
-        stats[s] = stat
 
         @pl.when(s == 0)
         def _():
@@ -377,32 +377,35 @@
         @pl.when(is_last)
         def _():
             mean[...] = mean[...] / SWEEPS
-
+            each(lambda d: column_spread(d).start())
+            pltpu.make_async_copy(quarter_of(my), columns.at[me, my], w_recv.at[0]).start()
+
+        run(effect_copies(s))
+        stats[s] = totals()
         each(lambda d: stat_spread(s, d).start())
         pltpu.make_async_copy(stats.at[s], gathered.at[s, pl.ds(own, 1), :], g_recv.at[s]).start()
-        run(effect_copies(s))
-
-        @pl.when(is_last)
+
+        @pl.when(s < SWEEPS - 1)
         def _():
-            each(lambda d: column_spread(d).start())
-            pltpu.make_async_copy(quarter_of(my), columns.at[me, my], w_recv.at[0]).start()
-
+            variances = update(s)
+            variance = variances[0]
+            for k in range(1, slab):
+                variance = jnp.where(my == k, variances[k], variance)
+            level[...] = jnp.broadcast_to(jnp.sqrt(variance / own_weight), (1, TILE))
+
+        return carry
+
+    def update(s):
         wait(effect_copies(s))
         pltpu.make_async_copy(gathered.at[s], gathered.at[s], g_recv.at[s]).wait()
         variances, _ = variances_of(gathered[s], slab)
-        state[...] = next_shrink(variances, [effects[s, k] for k in range(slab)], weights, shrink)
-        variance = variances[0]
-        for k in range(1, slab):
-            variance = jnp.where(my == k, variances[k], variance)
-        level[...] = jnp.broadcast_to(jnp.sqrt(variance / own_weight), (1, TILE))
-        return carry
+        state[...] = next_shrink(variances, [effects[s, k] for k in range(slab)], weights, state[...])
+        return variances
 
     lax.fori_loop(0, SWEEPS, sweep, 0)
-    new_shrink[...] = state[...].reshape(width)
-    pltpu.make_async_copy(columns, columns, w_recv.at[0]).wait()
-    live_total = variances_of(gathered[SWEEPS - 1], slab)[1]
     fetch.wait()
     chunks = quarter // TILE
+    pltpu.make_async_copy(columns, columns, w_recv.at[0]).wait()
 
     def arrange(g, sums):
         for c in range(chunks):
@@ -414,18 +417,20 @@
             sums = sums + value.astype(F32)
         return sums
 
-    sums = lax.fori_loop(0, samp, arrange, jnp.zeros((16, TILE), F32))
+    sums = lax.fori_loop(0, samp, arrange, jnp.zeros((16, TILE), F32), unroll=4)
     products = lax.dot_general(
         spread_columns[...], dose[...], (((1,), (1,)), ((), ())), preferred_element_type=F32)
     part = products - jnp.sum(sums, axis=1, keepdims=True)
     for k in range(slab):
         partial[k] = part[k : k + 1, :]
-    last = [pltpu.make_async_copy(partial.at[my], parts.at[my], local.at[2])]
+    last = [pltpu.make_async_copy(partial.at[my], parts.at[my], local.at[1])]
     for d in range(1, slab):
         last.append(pltpu.make_async_remote_copy(
             partial.at[lax.rem(my + d, slab)], parts.at[my], p_send.at[d], p_recv.at[d], **near(d)))
     run(last)
-    wait(last)
+    update(SWEEPS - 1)
+    new_shrink[...] = state[...].reshape(width)
+    live_total = variances_of(gathered[SWEEPS - 1], slab)[1]
     for s in range(SWEEPS):
         sent = gathered.at[s, pl.ds(0, everyone - 1), :]
         pltpu.make_async_copy(sent, sent, g_send.at[s]).wait()
@@ -435,6 +440,7 @@
         return carry
 
     lax.fori_loop(1, everyone, drain, 0)
+    wait(last)
     total = parts[0]
     for k in range(1, slab):
         total = total + parts[k]

time: 77.1 us -> 75.4 us (0.978)
  Pallas kernels: 76.3 us -> 74.6 us
    pallas_call x1, Pallas kernels: 75 us -> 73.2 us  [per_device(): pl.pallas_call(functools.partial(whole_kernel, samp, slab, slots, size),...]
where the time goes in v5:
time: 75.4 us; the launch traced here: 75.2 us
  Pallas kernels  74.6 us (99%)
    pallas_call x1, Pallas kernels, per_device(): pl.pallas_call(functools.partial(whole_kernel, samp, slab, slots, size),...  73.2 us

profile of v5, /device:TPU:1, one launch (start us, length us, event | category | flops | bytes accessed | tf_op | source)
XLA Modules:
  0.0 75.2 jit_solution(2730625887187710211)
XLA Ops:
  0.6 73.2 %sweeps.1 = (f32[1,1536]{1,0:T(1,128)}, f32[1536]{0:T(1024)}, f32[1,128]{1,0:T(1,128)}) custom-call(s32[2]{0:T(128)} %length.1, f32[4]{0:T(128)} %weights_ref.1, bf16[2,768,768]{2,1,0:T(8,128)(2,1)} %bitcast.2, f32[1,1536]{1,0:T(1,128)} %marginal.1, f32[2,1,1536]{2,1,0:T(1,128)} %normals.1, f32[1536]{0:T(1024)} %scale.1, bf16[128,12288]{1,0:T(8,128)(2,1)} %dosage.1), custom_call_target="tpu_custom_call" | custom-call | tf_op jit(solution)/shard_map/sweeps/pallas_call | solution.py:464
  73.9 1.3 %hand_over.1 = (f32[1,1536]{1,0:T(1,128)}, f32[1536]{0:T(1024)}, f32[1,128]{1,0:T(1,128)}) custom-call(f32[1,1536]{1,0:T(1,128)} %get-tuple-element.9.effects, f32[1536]{0:T(1024)} %get-tuple-element.10.shrink, f32[1,128]{1,0:T(1,128)} %get-tuple-element.11.scores), custom_call_target="tpu_custom_call" | custom-call | tf_op jit(solution)/shard_map/hand_over/pallas_call | solution.py:500

commit v6 on v5

--- a/solution.py
+++ b/solution.py
@@ -286,13 +286,17 @@
     return (pooled + 1.0) / (2.0 + jnp.sqrt(4.0 + 2.0 * rate * (pooled + 1.0)))
 
 
-def whole_kernel(samp, slab, slots, size, length, weights_ref, ld, marginal, normals, scale, dosage,
+def whole_kernel(samp, slab, slots, size, length, weights_ref, blocks, marginal, normals, scale, dosage,
                  mean, new_shrink, scores,
-                 work, diag, terms, turned, inverses, forward, draws, residual, blend, state, level, drawn, stats, effects, gathered, columns, spread_columns, dose, partial, parts,
+                 ld, work, diag, terms, turned, inverses, forward, draws, residual, blend, state, level, drawn, stats, effects, gathered, columns, spread_columns, dose, partial, parts,
                  e_send, e_recv, g_send, g_recv, w_send, w_recv, p_send, p_recv, local):
     me, my = lax.axis_index("samp"), lax.axis_index("slab")
     width = slots * size
     quarter = width // slab
+    bring = pltpu.make_async_copy(blocks, ld, local.at[3])
+    bring.start()
+    fetch = pltpu.make_async_copy(dosage, dose, local.at[0])
+    fetch.start()
     barrier = pltpu.get_barrier_semaphore()
 
     everyone = samp * slab
@@ -309,9 +313,7 @@
         pl.semaphore_signal(barrier, inc=1, device_id=peer_of(d), device_id_type=MESH)
         return carry
 
-    lax.fori_loop(1, everyone, greet, 0)
-    fetch = pltpu.make_async_copy(dosage, dose, local.at[0])
-    fetch.start()
+    lax.fori_loop(1, everyone, greet, 0, unroll=4)
     weights = [weights_ref[k] for k in range(slab)]
     own_weight = weights[0]
     for k in range(1, slab):
@@ -356,7 +358,7 @@
             act(far_first(d))
             return carry
 
-        lax.fori_loop(1, everyone, one, 0, unroll=4)
+        lax.fori_loop(1, everyone, one, 0, unroll=16)
 
     def sweep(s, carry):
         is_last = s == SWEEPS - 1
@@ -402,6 +404,7 @@
         state[...] = next_shrink(variances, [effects[s, k] for k in range(slab)], weights, state[...])
         return variances
 
+    bring.wait()
     lax.fori_loop(0, SWEEPS, sweep, 0)
     fetch.wait()
     chunks = quarter // TILE
@@ -468,9 +471,10 @@
             jax.ShapeDtypeStruct((width,), F32),
             jax.ShapeDtypeStruct((1, rows), F32),
         ),
-        in_specs=[smem, smem] + [vmem] * 4 + [pl.BlockSpec(memory_space=pl.ANY)],
+        in_specs=[smem, smem, pl.BlockSpec(memory_space=pl.ANY)] + [vmem] * 3 + [pl.BlockSpec(memory_space=pl.ANY)],
         out_specs=(vmem, vmem, vmem),
         scratch_shapes=[
+            pltpu.VMEM((slots, size, size), BF16),
             pltpu.VMEM((slots, size, size), F32),
             pltpu.VMEM((slots, TILE, TILE), F32),
             pltpu.VMEM((slots, 2, PIECES, TILE, size), BF16),

time: 75.4 us -> 74 us (0.981)
  Pallas kernels: 74.6 us -> 73.1 us
    pallas_call x1, Pallas kernels: 73.2 us -> 71.8 us  [per_device(): pl.pallas_call(functools.partial(whole_kernel, samp, slab, slots, size),...]
where the time goes in v6:
time: 74 us; the launch traced here: 73.8 us
  Pallas kernels  73.1 us (99%)
    pallas_call x1, Pallas kernels, per_device(): pl.pallas_call(functools.partial(whole_kernel, samp, slab, slots, size),...  71.8 us

profile of v6, /device:TPU:1, one launch (start us, length us, event | category | flops | bytes accessed | tf_op | source)
XLA Modules:
  0.0 73.8 jit_solution(17651706204451977469)
XLA Ops:
  0.6 71.8 %sweeps.1 = (f32[1,1536]{1,0:T(1,128)}, f32[1536]{0:T(1024)}, f32[1,128]{1,0:T(1,128)}) custom-call(s32[2]{0:T(128)} %length.1, f32[4]{0:T(128)} %weights_ref.1, bf16[2,768,768]{2,1,0:T(8,128)(2,1)} %bitcast.2, f32[1,1536]{1,0:T(1,128)} %marginal.1, f32[2,1,1536]{2,1,0:T(1,128)} %normals.1, f32[1536]{0:T(1024)} %scale.1, bf16[128,12288]{1,0:T(8,128)(2,1)} %dosage.1), custom_call_target="tpu_custom_call" | custom-call | tf_op jit(solution)/shard_map/sweeps/pallas_call | solution.py:467
  72.5 1.3 %hand_over.1 = (f32[1,1536]{1,0:T(1,128)}, f32[1536]{0:T(1024)}, f32[1,128]{1,0:T(1,128)}) custom-call(f32[1,1536]{1,0:T(1,128)} %get-tuple-element.9.effects, f32[1536]{0:T(1024)} %get-tuple-element.10.shrink, f32[1,128]{1,0:T(1,128)} %get-tuple-element.11.scores), custom_call_target="tpu_custom_call" | custom-call | tf_op jit(solution)/shard_map/hand_over/pallas_call | solution.py:504
